TPU v7x, 32 devices: a whole 2x2x4 slice. The times are simulated.
32 devices in a mesh: fn: 2 (over y), pts: 16 (over z, x, core).
Axes of the slice: x: 2, y: 2, z: 4, core: 2. Of those that a mesh axis runs over, the one named last changes fastest.
Arguments:
- points_in: bfloat16 [16, 4096, 128], P('pts', 'fn'), may hold values from -6 to 6
- geometry: bfloat16 [16, 4096, 128], P('pts', 'fn'), may hold values from -6 to 6
- functions: bfloat16 [2, 16, 2048, 128], P('fn', 'pts'), may hold values from -6 to 6
- presence: int32 [2, 16], P('fn', 'pts'), may hold values from 0 to 1, as said below
- fn_counts: int32 [2, 16], P('fn', 'pts'), may hold values from 512 to 2048
- item_counts: int32 [16], P('pts'), may hold values from 2048 to 4096, as said below
- cotangent: bfloat16 [16, 4096, 128], P('pts', 'fn'), may hold values from -6 to 6
- shared_weights: float32 [361728], replicated, may hold values from -4.4748737 to 4.4748737
- shared_momentum: float32 [361728], replicated, may hold values from -12288 to 12288
- shared_average: float32 [361728], replicated, may hold values from -4.4748737 to 4.4748737
- branch_weights: float32 [2, 33024], P('fn'), may hold values from -2 to 2
- branch_momentum: float32 [2, 33024], P('fn'), may hold values from -4344.464 to 4344.464
- branch_average: float32 [2, 33024], P('fn'), may hold values from -2 to 2
Outputs:
- output: bfloat16 [16, 4096, 128], P('pts', 'fn')
- input_grad: bfloat16 [16, 4096, 128], P('pts', 'fn')
- shared_weights_new: float32 [361728], replicated
- shared_momentum_new: float32 [361728], replicated
- shared_average_new: float32 [361728], replicated
- shared_copy: bfloat16 [361728], replicated
- branch_weights_new: float32 [2, 33024], P('fn')
- branch_momentum_new: float32 [2, 33024], P('fn')
- branch_average_new: float32 [2, 33024], P('fn')
- branch_copy: bfloat16 [2, 33024], P('fn')
- norm_grads: float32 [6, 128], replicated
Inputs may be any that keep to these rules, and one draw needn't show every extreme that they name: `presence`: each item has at least one present function, and one present function of each item uses all 2048 slots. `item_counts`: some item uses all 4096 slots.
All inputs are finite; a program needn't handle non-finite values.
Results may differ from a plain program's by a relative error of at most 0.012.
Values may be sent and summed in bfloat16 or wider, within the bound.
A program may use at most 128 MiB of HBM per device.

v0:
```python
import math

import jax
import jax.numpy as jnp
from jax import lax
from jax.sharding import PartitionSpec as P

D = 128
HEADS = 8
FF = 256
EXPERTS = 4
HEAD_DIM = 16


epsilon = 1e-05
far_below = -1e30
momentum_decay = 0.9
average_decay = 0.95


def merged(value, axis, join):
    pieces = jax.tree.map(lambda part: lax.all_gather(part, axis), value)
    head = jax.tree.map(lambda part: part[0], pieces)
    tail = jax.tree.map(lambda part: part[1:], pieces)
    so_far, _ = lax.scan(lambda so_far, share: (join(so_far, share), None), head, tail)
    return so_far


def split_shared(flat):
    shapes = [
        (D,),
        (D,),
        (D, D),
        (D, D),
        (D,),
        (D,),
        (D, 3 * D),
        (D, D),
        (D,),
        (D,),
        (D, EXPERTS),
        (EXPERTS, D, FF),
        (EXPERTS, FF, D),
    ]
    pieces = []
    offset = 0
    for segment_shape in shapes:
        segment_size = math.prod(segment_shape)
        pieces.append(flat[offset : offset + segment_size].reshape(segment_shape))
        offset = offset + segment_size
    return tuple(pieces)


def layer_norm(values, norm_gain, norm_bias):
    centred = values - jnp.mean(values, axis=-1, keepdims=True)
    spread = jnp.mean(centred * centred, axis=-1, keepdims=True)
    return centred * lax.rsqrt(spread + epsilon) * norm_gain + norm_bias


def norm_backward(values, norm_gain, norm_bias, upstream):
    pullback = jax.vjp(layer_norm, values, norm_gain, norm_bias)[1]
    return pullback(upstream)


def gelu_exact(values):
    return jax.nn.gelu(values, approximate=False)


def heads_view(values):
    return values.reshape(values.shape[:-1] + (HEADS, HEAD_DIM))


def feature_softmax(values):
    shaped = heads_view(values)
    powers = jnp.exp(shaped - jnp.max(shaped, axis=-1, keepdims=True))
    return (powers / jnp.sum(powers, axis=-1, keepdims=True)).reshape(values.shape)


def feature_softmax_back(soft, upstream):
    shaped = heads_view(soft)
    incoming = heads_view(upstream)
    inner_sum = jnp.sum(shaped * incoming, axis=-1, keepdims=True)
    return (shaped * (incoming - inner_sum)).reshape(soft.shape)


def masked_softmax(values, usable):
    masked = jnp.where(usable[..., None], values, far_below)
    column_max = jnp.max(masked, axis=-2, keepdims=True)
    powers = jnp.where(usable[..., None], jnp.exp(masked - column_max), 0.0)
    return powers / jnp.sum(powers, axis=-2, keepdims=True)


def summarize(weights, values):
    return jnp.einsum(
        "inhj,inhe->ihje",
        heads_view(weights),
        heads_view(values),
        preferred_element_type=jnp.float32,
    )


def apply_summary(weights, summary):
    mixed_rows = jnp.einsum(
        "inhj,ihje->inhe", heads_view(weights), summary, preferred_element_type=jnp.float32
    )
    return mixed_rows.reshape(weights.shape)


def apply_transposed(gradients, summary):
    rows_back = jnp.einsum(
        "inhe,ihje->inhj", heads_view(gradients), summary, preferred_element_type=jnp.float32
    )
    return rows_back.reshape(gradients.shape)


def combine_stats(first_part, second_part):
    joint_max = jnp.maximum(first_part[0], second_part[0])
    joint_sum = first_part[1] * jnp.exp(first_part[0] - joint_max) + second_part[1] * jnp.exp(
        second_part[0] - joint_max
    )
    return (joint_max, joint_sum)


def sgd_update(weights, momentum, average, gradient, step_rate):
    momentum_new = momentum_decay * momentum + gradient
    weights_new = weights - step_rate * (gradient + momentum_decay * momentum_new)
    average_new = average_decay * average + (1.0 - average_decay) * weights_new
    return (weights_new, momentum_new, average_new, weights_new.astype(jnp.bfloat16))


def local(
    points_in,
    geometry,
    functions,
    presence,
    fn_counts,
    item_counts,
    cotangent,
    shared_weights,
    shared_momentum,
    shared_average,
    branch_weights,
    branch_momentum,
    branch_average,
):
    fn_index = lax.axis_index("fn")
    item_rows = points_in.shape[0]
    row_count = points_in.shape[1]
    fn_points = functions.shape[2]
    positions = fn_index * row_count + lax.broadcasted_iota(jnp.int32, (item_rows, row_count), 1)
    item_usable = positions < item_counts[:, None]
    fn_usable = lax.broadcasted_iota(jnp.int32, (item_rows, fn_points), 1) < fn_counts[0][:, None]
    weighted = (presence[0] * fn_counts[0]).astype(jnp.float32)
    (
        gain_one,
        bias_one,
        cross_query,
        cross_output,
        gain_two,
        bias_two,
        self_qkv,
        self_output,
        gain_three,
        bias_three,
        router,
        expert_up,
        expert_down,
    ) = split_shared(shared_weights)
    cross_query_low = cross_query.astype(jnp.bfloat16)
    cross_output_low = cross_output.astype(jnp.bfloat16)
    self_qkv_low = self_qkv.astype(jnp.bfloat16)
    self_output_low = self_output.astype(jnp.bfloat16)
    router_low = router.astype(jnp.bfloat16)
    up_low = expert_up.astype(jnp.bfloat16)
    down_low = expert_down.astype(jnp.bfloat16)
    branch_gain = branch_weights[0, :D]
    branch_bias = branch_weights[0, D : 2 * D]
    kv_low = branch_weights[0, 2 * D :].reshape(D, 2 * D).astype(jnp.bfloat16)
    fn_data = functions[0].astype(jnp.float32)
    fn_hidden = layer_norm(fn_data, branch_gain, branch_bias).astype(jnp.bfloat16)
    fn_keyval = jnp.einsum("ipd,de->ipe", fn_hidden, kv_low, preferred_element_type=jnp.float32)
    fn_probs = masked_softmax(fn_keyval[..., :D], fn_usable)
    fn_weights = fn_probs.astype(jnp.bfloat16)
    fn_values = fn_keyval[..., D:].astype(jnp.bfloat16)
    fn_summary = summarize(fn_weights, fn_values)
    weighted_summary = weighted[:, None, None, None] * fn_summary
    count_total = lax.psum(weighted, "fn")
    mixed_total = lax.psum(weighted_summary, "fn")
    fn_share = weighted / count_total
    mixed_low = (mixed_total / count_total[:, None, None, None]).astype(jnp.bfloat16)
    points_float = points_in.astype(jnp.float32)
    norm_first = layer_norm(points_float, gain_one, bias_one).astype(jnp.bfloat16)
    cross_q = jnp.einsum(
        "ind,de->ine", norm_first, cross_query_low, preferred_element_type=jnp.float32
    )
    cross_soft = feature_softmax(cross_q)
    cross_weights = cross_soft.astype(jnp.bfloat16)
    cross_out = apply_summary(cross_weights, mixed_low).astype(jnp.bfloat16)
    after_cross = points_float + jnp.einsum(
        "ind,de->ine", cross_out, cross_output_low, preferred_element_type=jnp.float32
    )
    norm_second = layer_norm(after_cross, gain_two, bias_two).astype(jnp.bfloat16)
    self_qkv_out = jnp.einsum(
        "ind,de->ine", norm_second, self_qkv_low, preferred_element_type=jnp.float32
    )
    self_soft = feature_softmax(self_qkv_out[..., :D])
    self_weights = self_soft.astype(jnp.bfloat16)
    self_values = self_qkv_out[..., 2 * D :].astype(jnp.bfloat16)
    masked = jnp.where(item_usable[..., None], self_qkv_out[..., D : 2 * D], far_below)
    local_max = jnp.max(masked, axis=1)
    local_sum = jnp.sum(
        jnp.where(item_usable[..., None], jnp.exp(masked - local_max[:, None, :]), 0.0), axis=1
    )
    key_max, key_total = merged((local_max, local_sum), "fn", combine_stats)
    key_probs = (
        jnp.where(item_usable[..., None], jnp.exp(masked - key_max[:, None, :]), 0.0)
        / key_total[:, None, :]
    )
    key_weights = key_probs.astype(jnp.bfloat16)
    summary_part = summarize(key_weights, self_values)
    self_summary = lax.psum(summary_part.astype(jnp.bfloat16), "fn")
    self_out = apply_summary(self_weights, self_summary).astype(jnp.bfloat16)
    after_self = after_cross + jnp.einsum(
        "ind,de->ine", self_out, self_output_low, preferred_element_type=jnp.float32
    )
    norm_third = layer_norm(after_self, gain_three, bias_three).astype(jnp.bfloat16)
    logits = jnp.einsum("ind,de->ine", geometry, router_low, preferred_element_type=jnp.float32)
    powers = jnp.exp(logits - jnp.max(logits, axis=-1, keepdims=True))
    gate_probs = powers / jnp.sum(powers, axis=-1, keepdims=True)
    expert_pre = jnp.einsum("ind,edf->inef", norm_third, up_low, preferred_element_type=jnp.float32)
    expert_hidden = gelu_exact(expert_pre).astype(jnp.bfloat16)
    expert_result = jnp.einsum(
        "inef,efd->ined", expert_hidden, down_low, preferred_element_type=jnp.float32
    )
    output = (after_self + jnp.sum(gate_probs[..., None] * expert_result, axis=2)).astype(
        jnp.bfloat16
    )
    grad_out = cotangent.astype(jnp.float32)
    grad_expert = (gate_probs[..., None] * grad_out[:, :, None, :]).astype(jnp.bfloat16)
    grad_gates = jnp.sum(grad_out[:, :, None, :] * expert_result, axis=-1)
    grad_logits = (
        gate_probs * (grad_gates - jnp.sum(gate_probs * grad_gates, axis=-1, keepdims=True))
    ).astype(jnp.bfloat16)
    router_grad = jnp.einsum(
        "ind,ine->de", geometry, grad_logits, preferred_element_type=jnp.float32
    )
    down_grad = jnp.einsum(
        "inef,ined->efd", expert_hidden, grad_expert, preferred_element_type=jnp.float32
    )
    grad_hidden = jnp.einsum(
        "ined,efd->inef", grad_expert, down_low, preferred_element_type=jnp.float32
    )
    grad_pre = jax.vjp(gelu_exact, expert_pre)[1](grad_hidden)[0].astype(jnp.bfloat16)
    up_grad = jnp.einsum("ind,inef->edf", norm_third, grad_pre, preferred_element_type=jnp.float32)
    grad_norm_third = jnp.einsum(
        "inef,edf->ind", grad_pre, up_low, preferred_element_type=jnp.float32
    )
    grad_self_in, gain_three_grad, bias_three_grad = norm_backward(
        after_self, gain_three, bias_three, grad_norm_third
    )
    grad_after_self = grad_out + grad_self_in
    grad_self_proj = grad_after_self.astype(jnp.bfloat16)
    self_output_grad = jnp.einsum(
        "ind,ine->de", self_out, grad_self_proj, preferred_element_type=jnp.float32
    )
    grad_self_out = jnp.einsum(
        "ine,de->ind", grad_self_proj, self_output_low, preferred_element_type=jnp.float32
    ).astype(jnp.bfloat16)
    summary_grad = lax.psum(summarize(self_weights, grad_self_out).astype(jnp.bfloat16), "fn")
    grad_queries = feature_softmax_back(self_soft, apply_transposed(grad_self_out, self_summary))
    grad_key_weights = apply_transposed(self_values, summary_grad)
    local_correction = jnp.sum(key_probs * grad_key_weights, axis=1)
    correction = lax.psum(local_correction, "fn")
    grad_keys = key_probs * (grad_key_weights - correction[:, None, :])
    grad_values = apply_summary(key_weights, summary_grad)
    grad_qkv = jnp.concatenate([grad_queries, grad_keys, grad_values], axis=-1).astype(jnp.bfloat16)
    qkv_grad = jnp.einsum("ind,ine->de", norm_second, grad_qkv, preferred_element_type=jnp.float32)
    grad_norm_second = jnp.einsum(
        "ine,de->ind", grad_qkv, self_qkv_low, preferred_element_type=jnp.float32
    )
    grad_cross_in, gain_two_grad, bias_two_grad = norm_backward(
        after_cross, gain_two, bias_two, grad_norm_second
    )
    grad_after_cross = grad_after_self + grad_cross_in
    back_grad = jnp.concatenate(
        [
            gain_two_grad,
            bias_two_grad,
            qkv_grad.reshape(-1),
            self_output_grad.reshape(-1),
            gain_three_grad,
            bias_three_grad,
            router_grad.reshape(-1),
            up_grad.reshape(-1),
            down_grad.reshape(-1),
        ]
    )
    grad_cross_proj = grad_after_cross.astype(jnp.bfloat16)
    cross_output_grad = jnp.einsum(
        "ind,ine->de", cross_out, grad_cross_proj, preferred_element_type=jnp.float32
    )
    grad_cross_out = jnp.einsum(
        "ine,de->ind", grad_cross_proj, cross_output_low, preferred_element_type=jnp.float32
    ).astype(jnp.bfloat16)
    mixed_grad = lax.psum(summarize(cross_weights, grad_cross_out), "fn")
    grad_cross_q = feature_softmax_back(
        cross_soft, apply_transposed(grad_cross_out, mixed_low)
    ).astype(jnp.bfloat16)
    cross_query_grad = jnp.einsum(
        "ind,ine->de", norm_first, grad_cross_q, preferred_element_type=jnp.float32
    )
    grad_norm_first = jnp.einsum(
        "ine,de->ind", grad_cross_q, cross_query_low, preferred_element_type=jnp.float32
    )
    grad_points_in, gain_one_grad, bias_one_grad = norm_backward(
        points_float, gain_one, bias_one, grad_norm_first
    )
    input_grad = (grad_after_cross + grad_points_in).astype(jnp.bfloat16)
    fn_summary_grad = (fn_share[:, None, None, None] * mixed_grad).astype(jnp.bfloat16)
    grad_fn_weights = apply_transposed(fn_values, fn_summary_grad)
    fn_correction = jnp.sum(fn_probs * grad_fn_weights, axis=1, keepdims=True)
    grad_fn_keys = fn_probs * (grad_fn_weights - fn_correction)
    grad_fn_values = apply_summary(fn_weights, fn_summary_grad)
    grad_keyval = jnp.concatenate([grad_fn_keys, grad_fn_values], axis=-1).astype(jnp.bfloat16)
    kv_grad = jnp.einsum("ipd,ipe->de", fn_hidden, grad_keyval, preferred_element_type=jnp.float32)
    grad_fn_norm = jnp.einsum(
        "ipe,de->ipd", grad_keyval, kv_low, preferred_element_type=jnp.float32
    )
    ignored, fn_gain_grad, fn_bias_grad = norm_backward(
        fn_data, branch_gain, branch_bias, grad_fn_norm
    )
    branch_grad = jnp.concatenate([fn_gain_grad, fn_bias_grad, kv_grad.reshape(-1)])[None, :]
    front_grad = jnp.concatenate(
        [gain_one_grad, bias_one_grad, cross_query_grad.reshape(-1), cross_output_grad.reshape(-1)]
    )
    shared_total = lax.psum(jnp.concatenate([front_grad, back_grad]), ("fn", "pts"))
    branch_total = lax.psum(branch_grad, "pts")
    total_pieces = split_shared(shared_total)
    norm_grads = jnp.stack(
        [
            total_pieces[0],
            total_pieces[1],
            total_pieces[4],
            total_pieces[5],
            total_pieces[8],
            total_pieces[9],
        ]
    )
    item_total = item_rows * lax.axis_size("pts")
    shared_rate = 0.1 / math.sqrt(item_total * row_count * lax.axis_size("fn"))
    branch_rate = 0.1 / math.sqrt(item_total * fn_points)
    shared_new = sgd_update(
        shared_weights, shared_momentum, shared_average, shared_total, shared_rate
    )
    branch_new = sgd_update(
        branch_weights, branch_momentum, branch_average, branch_total, branch_rate
    )
    return (
        output,
        input_grad,
        shared_new[0],
        shared_new[1],
        shared_new[2],
        shared_new[3],
        branch_new[0],
        branch_new[1],
        branch_new[2],
        branch_new[3],
        norm_grads,
    )


def solution(mesh):
    return jax.shard_map(
        local,
        mesh=mesh,
        in_specs=(
            P("pts", "fn", None),
            P("pts", "fn", None),
            P("fn", "pts", None, None),
            P("fn", "pts"),
            P("fn", "pts"),
            P("pts"),
            P("pts", "fn", None),
            P(),
            P(),
            P(),
            P("fn", None),
            P("fn", None),
            P("fn", None),
        ),
        out_specs=(
            P("pts", "fn", None),
            P("pts", "fn", None),
            P(),
            P(),
            P(),
            P(),
            P("fn", None),
            P("fn", None),
            P("fn", None),
            P("fn", None),
            P(),
        ),
        check_vma=False,
    )
```

profile of v0, /device:TPU:0, one launch (start us, length us, event | category | flops | bytes accessed | tf_op | source)
XLA Modules:
  0.0 423.8 jit_solution(7566828766892300753)
XLA Ops:
  23.0 12.0 %all-reduce = (f32[1,8,16,16]{3,2,1,0:T(8,128)S(1)}, f32[1]{0:T(128)}) all-reduce(f32[1,8,16,16]{3,2,1,0:T(8,128)S(1)} %fusion.40, f32[1]{0:T(128)} %bitcast.10), channel_id=1, replica_groups=mesh['fn'=2,'pts'=16] {'fn'}, use_global_device_ids=true, to_apply=%region_4.5 | all-reduce | flops 2049 | bytes 16392 | tf_op jit(solution)/shard_map/psum | solution.py:188
  44.7 4.2 all-gather.3
  48.9 4.2 all-gather.2
  54.8 2.8 fusion.71
  59.4 8.2 %psum.58 = bf16[8,16,16]{2,1,0:T(8,128)(2,1)} all-reduce(bf16[8,16,16]{2,1,0:T(8,128)(2,1)} %convolution_convert_fusion.7), channel_id=1, replica_groups=mesh['fn'=2,'pts'=16] {'fn'}, use_global_device_ids=true, to_apply=%region_14.15 | all-reduce | flops 2048 | bytes 8192 | tf_op jit(solution)/shard_map/psum | solution.py:221
  78.1 2.0 copy.71
  80.1 2.1 convert_bitcast_fusion.2
  82.3 2.5 copy.72
  84.8 4.1 fusion.30
  88.9 19.0 %multiply_convert_fusion = (bf16[2048,4,256]{2,0,1:T(8,128)(2,1)S(1)}, f32[2048,4,256]{2,0,1:T(8,128)S(1)}) fusion(f32[2048,4,256]{2,0,1:T(8,128)S(1)} %get-tuple-element.112, u8[2048,256]{1,0:T(8,128)(4,1)S(1)} %get-tuple-element.60, u8[2048,256]{1,0:T(8,128)(4,1)S(1)} %get-tuple-element.59), kind=kLoop, calls=%fused_computation.16 | loop fusion | flops 146800640 | bytes 22020096 | tf_op jit(solution)/shard_map/convert_element_type | solution.py:231
  108.0 2.6 fusion.14
  110.7 4.6 %fusion.3 = bf16[1,2048,4,256]{3,1,2,0:T(8,128)(2,1)S(1)} fusion(f32[2048,4,256]{2,0,1:T(8,128)S(1)} %get-tuple-element.82, f32[2048,4,256]{2,0,1:T(8,128)S(1)} %get-tuple-element.112, bf16[4,256,128]{2,1,0:T(8,128)(2,1)S(1)} %bitcast.423, f32[2048,128]{1,0:T(8,128)S(1)} %copy-done.42, f32[2048,4]{0,1:T(4,128)S(1)} %copy-done.75), kind=kOutput, calls=%fused_computation.10 | convolution fusion | flops 568328192 | bytes 22315008 | tf_op jit(solution)/shard_map/ined,efd->inef/dot_general | solution.py:250
  117.3 2.8 fusion.152
  120.1 2.6 copy.73
  122.6 2.1 fusion.63
  124.8 2.8 fusion.142
  132.2 8.9 %psum.59 = bf16[8,16,16]{2,1,0:T(8,128)(2,1)S(1)} all-reduce(bf16[8,16,16]{2,1,0:T(8,128)(2,1)S(1)} %convolution_convert_fusion.6), channel_id=1, replica_groups=mesh['fn'=2,'pts'=16] {'fn'}, use_global_device_ids=true, to_apply=%region_25.26 | all-reduce | flops 2048 | bytes 8192 | tf_op jit(solution)/shard_map/psum | solution.py:269
  142.4 2.2 convolution_convert_fusion.3
  147.0 4.9 %psum.60 = f32[128]{0:T(128)S(1)} all-reduce(f32[128]{0:T(128)S(1)} %fusion.66), channel_id=1, replica_groups=mesh['fn'=2,'pts'=16] {'fn'}, use_global_device_ids=true, to_apply=%region_27.28 | all-reduce | flops 128 | bytes 1024 | tf_op jit(solution)/shard_map/psum | solution.py:273
  153.7 2.0 multiply_convert_fusion.5
  155.8 2.2 fusion.151
  164.8 7.4 %psum.62 = f32[1,8,16,16]{3,2,1,0:T(8,128)S(1)} all-reduce(f32[1,8,16,16]{3,2,1,0:T(8,128)S(1)} %convolution_bitcast_fusion.10), channel_id=1, replica_groups=mesh['fn'=2,'pts'=16] {'fn'}, use_global_device_ids=true, to_apply=%region_42.43 | all-reduce | flops 2048 | bytes 16384 | tf_op jit(solution)/shard_map/psum | solution.py:305
  176.4 2.0 fusion.57
  180.9 4.4 %fusion.35 = f32[4,128,256]{1,2,0:T(8,128)} fusion(bf16[1,2048,4,256]{3,1,2,0:T(8,128)(2,1)} %copy-done.16, f32[1,2048,128]{1,2,0:T(8,128)S(1)} %copy-done.7, f32[128]{0:T(128)S(1)} %copy-done.118, f32[128]{0:T(128)S(1)} %copy-done.109, f32[2048]{0:T(1024)S(1)} %copy-done.83, f32[2048]{0:T(1024)S(1)} %copy-done.72), kind=kOutput, calls=%fused_computation.82 | convolution fusion | flops 538181632 | bytes 5784576 | tf_op jit(solution)/shard_map/ind,inef->edf/dot_general | solution.py:254
  190.5 3.4 fusion.150
  195.7 3.2 fusion.19
  227.3 2.2 copy.87
  231.5 37.8 %all-reduce.6.cloned.1.call-done = f32[1,33024]{1,0:T(1,128)} async-done(((f32[1,33024]{1,0:T(1,128)}), f32[1,33024]{1,0:T(1,128)}) %all-reduce.6.cloned.1.call-update) | async-done | bytes 132112 | tf_op jit(solution)/shard_map/psum | solution.py:337
  269.3 2.1 fusion.140
  272.3 135.6 %all-reduce.4.cloned.1.call-done = f32[361728]{0:T(1024)} async-done(((f32[361728]{0:T(1024)}), f32[361728]{0:T(1024)}) %all-reduce.4.cloned.1.call-update) | async-done | bytes 1446928 | tf_op jit(solution)/shard_map/psum | solution.py:336
  407.9 3.5 fusion.141
  412.5 2.7 multiply_add_fusion
  (356 shorter events, 101.7 us)
Async XLA Ops:
  7.2 68.0 %copy-start = (bf16[1,2048,128]{2,1,0:T(8,128)(2,1)S(1)}, bf16[1,2048,128]{2,1,0:T(8,128)(2,1)}, u32[]{:S(2)}) copy-start(bf16[1,2048,128]{2,1,0:T(8,128)(2,1)} %param.14) | copy-start | bytes 1572868
  7.2 262.1 %all-reduce.6.cloned.1.call-start = ((), (), s32[]{:S(2)}) async-start(), calls=%async_computation.1 | async-start | bytes 264192 | tf_op jit(solution)/shard_map/psum | solution.py:337
  8.6 29.4 %copy-start.102 = (f32[128]{0:T(128)}, f32[128]{0:T(128)S(1)}, u32[]{:S(2)}) copy-start(f32[128]{0:T(128)S(1)} %get-tuple-element.95) | copy-start | bytes 1540
  8.6 29.4 %copy-start.112 = (f32[128]{0:T(128)}, f32[128]{0:T(128)S(1)}, u32[]{:S(2)}) copy-start(f32[128]{0:T(128)S(1)} %get-tuple-element.94) | copy-start | bytes 1540
  10.1 25.9 %copy-start.38 = (bf16[361728]{0:T(1024)(128)(2,1)}, bf16[361728]{0:T(1024)(128)(2,1)S(1)}, u32[]{:S(2)}) copy-start(bf16[361728]{0:T(1024)(128)(2,1)S(1)} %convert.40) | copy-start | bytes 2170372
  17.7 17.3 %copy-start.24 = (bf16[2048,128]{0,1:T(8,128)(2,1)}, bf16[2048,128]{0,1:T(8,128)(2,1)S(1)}, u32[]{:S(2)}) copy-start(bf16[2048,128]{0,1:T(8,128)(2,1)S(1)} %fusion.73) | copy-start | bytes 1572868
  20.5 16.7 %copy-start.97 = (f32[128]{0:T(128)}, f32[128]{0:T(128)S(1)}, u32[]{:S(2)}) copy-start(f32[128]{0:T(128)S(1)} %fusion.79) | copy-start | bytes 1540
  21.7 15.6 %copy-start.104 = (f32[128]{0:T(128)}, f32[128]{0:T(128)S(1)}, u32[]{:S(2)}) copy-start(f32[128]{0:T(128)S(1)} %fusion.82) | copy-start | bytes 1540
  41.4 12.3 %copy-start.91 = (pred[2048]{0:T(1024)(128)(4,1)}, pred[2048]{0:T(1024)(128)(4,1)S(1)}, u32[]{:S(2)}) copy-start(pred[2048]{0:T(1024)(128)(4,1)S(1)} %add_compare_fusion) | copy-start | bytes 6148
  44.7 24.4 %copy-start.12 = (f32[1,2048,128]{1,2,0:T(8,128)}, f32[1,2048,128]{1,2,0:T(8,128)S(1)}, u32[]{:S(2)}) copy-start(f32[1,2048,128]{1,2,0:T(8,128)S(1)} %get-tuple-element.85) | copy-start | bytes 3145732
  71.0 53.8 %copy-start.6 = (f32[1,2048,128]{1,2,0:T(8,128)}, f32[1,2048,128]{1,2,0:T(8,128)S(1)}, u32[]{:S(2)}) copy-start(f32[1,2048,128]{1,2,0:T(8,128)S(1)} %get-tuple-element.111) | copy-start | bytes 3145732
  88.9 19.1 %copy-start.35 = (f32[2048,128]{0,1:T(8,128)S(1)}, f32[2048,128]{0,1:T(8,128)}, u32[]{:S(2)}) copy-start(f32[2048,128]{0,1:T(8,128)} %convert_bitcast_fusion.2) | copy-start | bytes 3145732
  88.9 19.1 %copy-start.65 = (bf16[131072]{0:T(1024)(128)(2,1)S(1)}, bf16[131072]{0:T(1024)(128)(2,1)}, u32[]{:S(2)}) copy-start(bf16[131072]{0:T(1024)(128)(2,1)} %get-tuple-element.100) | copy-start | bytes 786436
  88.9 19.1 %copy-start.75 = (f32[2048,4]{0,1:T(4,128)S(1)}, f32[2048,4]{0,1:T(4,128)}, u32[]{:S(2)}) copy-start(f32[2048,4]{0,1:T(4,128)} %fusion.113) | copy-start | bytes 98308
  129.8 15.4 %copy-start.92 = (pred[2048]{0:T(1024)(128)(4,1)S(1)}, pred[2048]{0:T(1024)(128)(4,1)}, u32[]{:S(2)}) copy-start(pred[2048]{0:T(1024)(128)(4,1)} %copy-done.91) | copy-start | bytes 6148
  129.9 15.4 %copy-start.107 = (f32[128]{0:T(128)S(1)}, f32[128]{0:T(128)}, u32[]{:S(2)}) copy-start(f32[128]{0:T(128)} %get-tuple-element.104) | copy-start | bytes 1540
  142.4 13.4 %copy-start.62 = (bf16[128,384]{1,0:T(8,128)(2,1)S(1)}, bf16[128,384]{1,0:T(8,128)(2,1)}, u32[]{:S(2)}) copy-start(bf16[128,384]{1,0:T(8,128)(2,1)} %copy-done.61) | copy-start | bytes 294916
  161.1 12.9 %copy-start.80 = (pred[2048]{0:T(1024)(128)(4,1)S(1)}, pred[2048]{0:T(1024)(128)(4,1)}, u32[]{:S(2)}) copy-start(pred[2048]{0:T(1024)(128)(4,1)} %copy-done.79) | copy-start | bytes 6148
  161.1 12.9 %copy-start.98 = (f32[128]{0:T(128)S(1)}, f32[128]{0:T(128)}, u32[]{:S(2)}) copy-start(f32[128]{0:T(128)} %copy-done.97) | copy-start | bytes 1540
  161.2 12.9 %copy-start.105 = (f32[128]{0:T(128)S(1)}, f32[128]{0:T(128)}, u32[]{:S(2)}) copy-start(f32[128]{0:T(128)} %copy-done.104) | copy-start | bytes 1540
  164.5 11.9 %copy-start.64 = (bf16[128,256]{1,0:T(8,128)(2,1)S(1)}, bf16[128,256]{1,0:T(8,128)(2,1)}, u32[]{:S(2)}) copy-start(bf16[128,256]{1,0:T(8,128)(2,1)} %copy-done.63) | copy-start | bytes 196612
  164.5 11.9 %copy-start.82 = (f32[2048]{0:T(1024)S(1)}, f32[2048]{0:T(1024)}, u32[]{:S(2)}) copy-start(f32[2048]{0:T(1024)} %copy-done.81) | copy-start | bytes 24580
  164.5 11.9 %copy-start.96 = (f32[2048]{0:T(1024)S(1)}, f32[2048]{0:T(1024)}, u32[]{:S(2)}) copy-start(f32[2048]{0:T(1024)} %copy-done.95) | copy-start | bytes 24580
  180.6 227.3 %all-reduce.4.cloned.1.call-start = ((), (), s32[]{:S(2)}) async-start(), calls=%async_computation | async-start | bytes 2899968 | tf_op jit(solution)/shard_map/psum | solution.py:336
  201.2 19.7 %copy-start.106 = (f32[512]{0:T(512)S(1)}, f32[512]{0:T(512)}, u32[]{:S(2)}) copy-start(f32[512]{0:T(512)} %reshape.1117) | copy-start | bytes 6148
  203.8 18.5 %copy-start.41 = (f32[64,2,8,128]{3,1,2,0:T(2,128)S(1)}, f32[64,2,8,128]{3,1,2,0:T(2,128)}, u32[]{:S(2)}) copy-start(f32[64,2,8,128]{3,1,2,0:T(2,128)} %copy.99) | copy-start | bytes 1572868
  203.8 20.4 %copy-start.53 = (f32[4,256,128]{2,1,0:T(8,128)S(1)}, f32[4,256,128]{2,1,0:T(8,128)}, u32[]{:S(2)}) copy-start(f32[4,256,128]{2,1,0:T(8,128)} %fusion.19) | copy-start | bytes 1572868
  203.8 22.4 %copy-start.101 = (f32[128]{0:T(128)S(1)}, f32[128]{0:T(128)}, u32[]{:S(2)}) copy-start(f32[128]{0:T(128)} %copy-done.99) | copy-start | bytes 1540
  222.3 47.1 %copy-start.49 = (f32[1,33024]{1,0:T(1,128)S(1)}, f32[1,33024]{1,0:T(1,128)}, u32[]{:S(2)}) copy-start(f32[1,33024]{1,0:T(1,128)} %param.23) | copy-start | bytes 396292
  224.2 47.2 %copy-start.70 = (f32[1,33024]{1,0:T(1,128)S(1)}, f32[1,33024]{1,0:T(1,128)}, u32[]{:S(2)}) copy-start(f32[1,33024]{1,0:T(1,128)} %param.25) | copy-start | bytes 396292
  227.3 180.5 %copy-start.17 = (f32[361728]{0:T(1024)S(1)}, f32[361728]{0:T(1024)}, u32[]{:S(2)}) copy-start(f32[361728]{0:T(1024)} %param.20) | copy-start | bytes 4340740
  271.4 143.7 %copy-start.50 = (f32[1,33024]{1,0:T(1,128)}, f32[1,33024]{1,0:T(1,128)S(1)}, u32[]{:S(2)}) copy-start(f32[1,33024]{1,0:T(1,128)S(1)} %get-tuple-element.74) | copy-start | bytes 396292
  (89 other events, 350.4 us)
Sparse Core Ops, SparseCore 0:
  180.7 88.5 all-reduce.5
  275.2 132.5 all-reduce.3
where the time goes:
time: 432 us; the launch traced here: 424 us
  waiting for transfers between devices  173 us (40%)
  local copies, waits for them, and re-layouts  63.9 us (15%)
  other arithmetic  63.6 us (15%)
  matrix products  54 us (12%)
  blocking collectives  49.9 us (12%)
  between operations  18.7 us (4%)
    psum x1, waiting for transfers between devices, local(): lax.psum(jnp.concatenate([front_grad, back_grad]), ('fn', 'pts'))  136 us
    unnamed x256, local copies, waits for them, and re-layouts  40.7 us
    psum x1, waiting for transfers between devices, local(): branch_total = lax.psum(branch_grad, 'pts')  37.8 us
    convert_element_type x1, other arithmetic, local(): expert_hidden = gelu_exact(expert_pre).astype(jnp.bfloat16)  19 us
    psum x1, blocking collectives, local(): mixed_total = lax.psum(weighted_summary, 'fn')  12 us
    psum x1, blocking collectives, local(): lax.psum(summarize(self_weights, grad_self_out).astype(jnp.bfloat16), 'fn')  8.89 us
  transfers between devices with their start and end apart: 2, of which 2 were waited for; matrix products, arithmetic and copies ran while one was open for 13% of the time, Pallas kernels for 0%

commit v1 on v0

v1 whole, which is shorter than its diff:
```python
import functools
import math

import jax
import jax.numpy as jnp
from jax import lax
from jax.experimental import pallas as pl
from jax.experimental.pallas import tpu as pltpu
from jax.sharding import PartitionSpec as P

D = 128
HEADS = 8
FF = 256
EXPERTS = 4
HEAD_DIM = 16
HIDDEN = EXPERTS * FF

epsilon = 1e-05
far_below = -1e30
momentum_decay = 0.9
average_decay = 0.95

F32 = jnp.float32
BF16 = jnp.bfloat16
MESH = pl.DeviceIdType.MESH

ROW_GAIN_ONE, ROW_BIAS_ONE = 0, 1
ROW_QUERY = 2
ROW_CROSS_OUT = ROW_QUERY + D
ROW_GAIN_TWO = ROW_CROSS_OUT + D
ROW_BIAS_TWO = ROW_GAIN_TWO + 1
ROW_QKV = ROW_BIAS_TWO + 1
ROW_SELF_OUT = ROW_QKV + 3 * D
ROW_GAIN_THREE = ROW_SELF_OUT + D
ROW_BIAS_THREE = ROW_GAIN_THREE + 1
ROW_ROUTER = ROW_BIAS_THREE + 1
ROW_UP = ROW_ROUTER + EXPERTS
ROW_DOWN = ROW_UP + 2 * D * EXPERTS
SHARED_ROWS = ROW_DOWN + HIDDEN
BRANCH_ROWS = 2 + 2 * D

EXPERT_ROWS = 2 * HIDDEN
T_QUERY, T_CROSS_OUT, T_QKV, T_SELF_OUT = 0, D, 2 * D, 5 * D
T_SMALL = 6 * D
TAIL_ROWS = T_SMALL + 32
B_SMALL = 2 * D
BRANCH_SENT = B_SMALL + 16


def dot(a, b):
    return jnp.dot(a, b, preferred_element_type=F32)


def dot_points(a, b):
    return lax.dot_general(a, b, (((1,), (1,)), ((), ())), preferred_element_type=F32)


class Level:
    def __init__(self, size, index, member):
        self.size, self.index, self.member = size, index, member


def split_rows(rows, size):
    step = 16
    while rows % step or rows // step > size:
        step += 16
    return step, rows // step


class Reduction:
    def __init__(self, sizes, rows):
        self.sizes, self.rows = sizes, rows
        self.steps, self.owners = [], []
        for size in sizes:
            step, owners = split_rows(rows, size)
            self.steps.append(step)
            self.owners.append(owners)
            rows = step

    def scratch(self):
        shapes = [pltpu.VMEM((self.rows, D), BF16), pltpu.VMEM((self.rows, D), BF16)]
        for at, size in enumerate(self.sizes):
            shapes.append(pltpu.VMEM((size - 1, self.steps[at], D), BF16))
            shapes.append(pltpu.VMEM((self.steps[at], D), BF16))
            shapes += [pltpu.SemaphoreType.DMA((size - 1,))] * 4
        return shapes

    def bind(self, refs, levels):
        self.source, self.total = refs[0], refs[1]
        self.parts = [refs[2 + 6 * at : 8 + 6 * at] for at in range(len(self.sizes))]
        self.levels = levels

    def base(self, at):
        start = 0
        for upper in range(at):
            start = start + self.levels[upper].index * self.steps[upper]
        return start

    def guard(self, at, own):
        condition = None
        for upper in range(at + 1 if own else at):
            if self.owners[upper] < self.sizes[upper]:
                here = self.levels[upper].index < self.owners[upper]
                condition = here if condition is None else jnp.logical_and(condition, here)
        return condition

    def when(self, condition, body):
        if condition is None:
            body()
        else:
            pl.when(condition)(body)

    def each(self, at, body):
        def step(k, carry):
            body(k)
            return carry

        lax.fori_loop(1, self.sizes[at], step, 0)

    def scatter_copy(self, at, k):
        level, step = self.levels[at], self.steps[at]
        peer = (level.index + k) % level.size
        source = self.source if at == 0 else self.parts[at - 1][1]
        start = jnp.where(peer < self.owners[at], peer, 0) if self.owners[at] < level.size else peer
        received, _, send, receive = self.parts[at][:4]
        return peer, pltpu.make_async_remote_copy(
            src_ref=source.at[pl.ds(pl.multiple_of(start * step, 16), step), :],
            dst_ref=received.at[k - 1],
            send_sem=send.at[k - 1],
            recv_sem=receive.at[k - 1],
            device_id=level.member(peer),
            device_id_type=MESH,
        )

    def peer_guard(self, at, index):
        return None if self.owners[at] == self.sizes[at] else index < self.owners[at]

    def scatter(self, at):
        def go():
            def one(k):
                peer, copy = self.scatter_copy(at, k)
                self.when(self.peer_guard(at, peer), copy.start)

            self.each(at, one)

        self.when(self.guard(at, False), go)

    def add(self, at):
        level, step = self.levels[at], self.steps[at]

        def go():
            self.each(at, lambda k: self.scatter_copy(at, k)[1].wait_recv())
            received = self.parts[at][0]
            source = self.source if at == 0 else self.parts[at - 1][1]
            own = source[pl.ds(pl.multiple_of(level.index * step, 16), step), :].astype(F32)
            total = lax.fori_loop(
                0, level.size - 1, lambda k, so_far: so_far + received[k].astype(F32), own
            ).astype(BF16)
            if at + 1 < len(self.sizes):
                self.parts[at][1][...] = total
            else:
                start = pl.multiple_of(self.base(at) + level.index * step, 16)
                self.total[pl.ds(start, step), :] = total

        self.when(self.guard(at, True), go)

    def gather_copy(self, at, k, owner):
        level, step = self.levels[at], self.steps[at]
        start = pl.multiple_of(self.base(at) + owner * step, 16)
        send, receive = self.parts[at][4:]
        return pltpu.make_async_remote_copy(
            src_ref=self.total.at[pl.ds(start, step), :],
            dst_ref=self.total.at[pl.ds(start, step), :],
            send_sem=send.at[k - 1],
            recv_sem=receive.at[k - 1],
            device_id=level.member((level.index + k) % level.size),
            device_id_type=MESH,
        )

    def gather(self, at):
        def go():
            self.each(at, lambda k: self.gather_copy(at, k, self.levels[at].index).start())

        self.when(self.guard(at, True), go)

    def collect(self, at):
        level = self.levels[at]

        def go():
            def one(k):
                owner = (level.index + level.size - k) % level.size
                self.when(self.peer_guard(at, owner), self.gather_copy(at, k, owner).wait_recv)

            self.each(at, one)

        self.when(self.guard(at, False), go)

    def drain(self):
        for at in range(len(self.sizes)):

            def scattered(at=at):
                def one(k):
                    peer, copy = self.scatter_copy(at, k)
                    self.when(self.peer_guard(at, peer), copy.wait_send)

                self.each(at, one)

            def gathered(at=at):
                self.each(at, lambda k: self.gather_copy(at, k, self.levels[at].index).wait_send())

            self.when(self.guard(at, False), scattered)
            self.when(self.guard(at, True), gathered)


def near(pts):
    return 4 if pts % 4 == 0 else 1


def plan(fns, pts):
    inner = near(pts)
    two = [fns * inner, pts // inner]
    expert = Reduction(two, EXPERT_ROWS)
    if fns * pts <= 32:
        return expert, Reduction([fns * pts], TAIL_ROWS), Reduction([pts], BRANCH_SENT)
    return expert, Reduction(two, TAIL_ROWS), Reduction([inner, pts // inner], BRANCH_SENT)


def layer_norm(values):
    centred = values - jnp.mean(values, axis=0, keepdims=True)
    spread = jnp.mean(centred * centred, axis=0, keepdims=True)
    inverse = lax.rsqrt(spread + epsilon)
    return centred * inverse, inverse


def norm_back(normed, inverse, gain, upstream):
    scaled = upstream * gain
    first = jnp.mean(scaled, axis=0, keepdims=True)
    second = jnp.mean(scaled * normed, axis=0, keepdims=True)
    return (scaled - first - normed * second) * inverse


def heads_view(values):
    return values.reshape(HEADS, HEAD_DIM, values.shape[-1])


def feature_softmax(values):
    shaped = heads_view(values)
    powers = jnp.exp(shaped - jnp.max(shaped, axis=1, keepdims=True))
    return (powers * (1.0 / jnp.sum(powers, axis=1, keepdims=True))).reshape(values.shape)


def feature_softmax_back(soft, upstream):
    shaped, incoming = heads_view(soft), heads_view(upstream)
    inner = jnp.sum(shaped * incoming, axis=1, keepdims=True)
    return (shaped * (incoming - inner)).reshape(soft.shape)


def lane_fold(values, join):
    out = values[:, :D]
    for at in range(D, values.shape[1], D):
        out = join(out, values[:, at : at + D])
    return out


def step_kernel(fns, pts, block, *refs):
    refs = list(refs)

    def take(n):
        got = refs[:n]
        del refs[:n]
        return got

    (
        presence,
        fn_counts,
        item_counts,
        points_hbm,
        geometry_hbm,
        functions_hbm,
        cotangent_hbm,
        shared_hbm,
        branch_hbm,
    ) = take(9)
    output_hbm, input_grad_hbm, shared_grad_hbm, branch_grad_hbm = take(4)
    points_v, geometry_v, functions_v, cotangent_v, shared_v, branch_v = take(6)
    (
        query_w,
        query_t,
        cross_w,
        cross_t,
        qkv_w,
        qkv_t,
        self_w,
        self_t,
        up_w,
        up_t,
        down_w,
        down_t,
        kv_w,
        kv_t,
        router_t,
    ) = take(15)
    (
        fn_hidden,
        fn_powers,
        fn_low,
        fn_values,
        hidden_one,
        cross_soft,
        cross_out,
        after_cross,
        hidden_two,
        self_soft,
        key_powers,
        key_low,
        self_values,
        self_out_v,
        cot_t,
        gates_v,
        g_self,
        g_self_out,
        g_queries,
        g_cross,
        g_cross_out,
        hidden_v,
        pre_v,
    ) = take(23)
    up_sum, down_sum, norm_sums, out_v, in_grad_v, shared_out, branch_out = take(7)
    sent, got = take(2)
    local_sem, x_send, x_recv = take(3)
    expert, tail, branch = plan(fns, pts)
    expert_refs = take(len(expert.scratch()))
    tail_refs = take(len(tail.scratch()))
    branch_refs = take(len(branch.scratch()))
    assert not refs

    fn, pt = lax.axis_index("fn"), lax.axis_index("pts")
    inner = near(pts)
    outer_at, inner_at = pt // inner, pt % inner
    near_level = Level(
        fns * inner, fn * inner + inner_at, lambda j: (j // inner, outer_at * inner + j % inner)
    )
    far_level = Level(pts // inner, outer_at, lambda j: (fn, j * inner + inner_at))
    world = Level(fns * pts, fn * pts + pt, lambda j: (j // pts, j % pts))
    item_level = Level(pts, pt, lambda j: (fn, j))
    core_level = Level(inner, inner_at, lambda j: (fn, outer_at * inner + j))
    expert.bind(expert_refs, [near_level, far_level])
    if fns * pts <= 32:
        tail.bind(tail_refs, [world])
        branch.bind(branch_refs, [item_level])
        greeted = [world]
    else:
        tail.bind(tail_refs, [near_level, far_level])
        branch.bind(branch_refs, [core_level, far_level])
        greeted = [near_level, far_level]

    rows = points_v.shape[0]
    fn_rows = functions_v.shape[0]
    blocks = rows // block
    fn_blocks = fn_rows // block

    loads = []
    for at, (source, target) in enumerate(
        [
            (branch_hbm, branch_v),
            (functions_hbm, functions_v),
            (shared_hbm, shared_v),
            (points_hbm, points_v),
            (geometry_hbm, geometry_v),
            (cotangent_hbm, cotangent_v),
        ]
    ):
        loads.append(pltpu.make_async_copy(source, target, local_sem.at[at]))
        loads[-1].start()

    barrier = pltpu.get_barrier_semaphore()
    for level in greeted:

        def greet(k, carry, level=level):
            pl.semaphore_signal(
                barrier,
                inc=1,
                device_id=level.member((level.index + k) % level.size),
                device_id_type=MESH,
            )
            return carry

        lax.fori_loop(1, level.size, greet, 0)

    def exchange(at):
        return pltpu.make_async_remote_copy(
            src_ref=sent.at[at],
            dst_ref=got.at[at],
            send_sem=x_send.at[at],
            recv_sem=x_recv.at[at],
            device_id=((fn + 1) % fns, pt),
            device_id_type=MESH,
        )

    row_at = lax.broadcasted_iota(jnp.int32, (D, D), 0)
    column_at = lax.broadcasted_iota(jnp.int32, (D, D), 1)
    same_head = row_at // HEAD_DIM == column_at // HEAD_DIM
    diagonal = row_at == column_at

    def diagonal_blocks(full):
        return jnp.where(same_head, full, 0.0)

    def folded(full):
        kept = diagonal_blocks(full)
        out = kept[:HEAD_DIM]
        for head in range(1, HEADS):
            out = out + kept[head * HEAD_DIM : (head + 1) * HEAD_DIM]
        return out

    def unfolded(compact):
        return diagonal_blocks(jnp.concatenate([compact] * HEADS, axis=0))

    def to_row(column):
        return jnp.sum(jnp.where(diagonal, column, 0.0), axis=0, keepdims=True)

    def to_column(row):
        return jnp.sum(jnp.where(diagonal, row, 0.0), axis=1, keepdims=True)

    def span(b):
        return pl.ds(pl.multiple_of(b * block, block), block)

    def zeros(ref):
        ref[...] = jnp.zeros_like(ref)

    loads[0].wait()
    kv = jnp.concatenate(
        [branch_v[pl.ds(2, D, stride=2), :], branch_v[pl.ds(3, D, stride=2), :]], axis=1
    ).astype(BF16)
    kv_w[...] = kv
    kv_t[...] = kv.T
    branch_gain = to_column(branch_v[0:1, :])
    branch_bias = to_column(branch_v[1:2, :])
    fn_count = fn_counts[0, 0]
    fn_weight = (presence[0, 0] * fn_count).astype(F32)
    loads[1].wait()

    def fn_usable(b):
        at = lax.broadcasted_iota(jnp.int32, (1, block), 1) + b * block
        return at < fn_count

    def encode(b, so_far):
        normed, _ = layer_norm(functions_v[span(b), :].astype(F32).T)
        hidden = (normed * branch_gain + branch_bias).astype(BF16)
        fn_hidden[:, span(b)] = hidden
        keyval = dot(kv_t[...], hidden)
        keys = jnp.where(fn_usable(b), keyval[:D], far_below)
        fn_powers[:, span(b)] = keys
        fn_values[:, span(b)] = keyval[D:].astype(BF16)
        return jnp.maximum(so_far, lane_fold(keys, jnp.maximum))

    fn_max = jnp.max(
        lax.fori_loop(0, fn_blocks, encode, jnp.full((D, D), far_below, F32)), axis=1, keepdims=True
    )

    def fn_total(b, so_far):
        powers = jnp.where(fn_usable(b), jnp.exp(fn_powers[:, span(b)] - fn_max), 0.0)
        fn_powers[:, span(b)] = powers
        low = powers.astype(BF16)
        fn_low[:, span(b)] = low
        return (
            so_far[0] + lane_fold(powers, jnp.add),
            so_far[1] + dot_points(low, fn_values[:, span(b)]),
        )

    nothing = jnp.zeros((D, D), F32)
    totals, fn_sum = lax.fori_loop(0, fn_blocks, fn_total, (nothing, nothing))
    fn_scale = 1.0 / jnp.sum(totals, axis=1, keepdims=True)
    fn_summary = diagonal_blocks(fn_sum * fn_scale)
    weighted_summary = fn_weight * folded(fn_summary)
    sent[0, 0:HEAD_DIM, :] = weighted_summary
    sent[0, HEAD_DIM : HEAD_DIM + 8, :] = jnp.full((8, D), fn_weight, F32)
    pl.semaphore_wait(barrier, sum(level.size - 1 for level in greeted))
    exchange(0).start()

    loads[2].wait()

    def shared_rows(start, stride=1):
        return shared_v[pl.ds(start, D, stride=stride), :].astype(BF16)

    query_w[...] = shared_rows(ROW_QUERY)
    query_t[...] = shared_rows(ROW_QUERY).T
    cross_w[...] = shared_rows(ROW_CROSS_OUT)
    cross_t[...] = shared_rows(ROW_CROSS_OUT).T
    self_w[...] = shared_rows(ROW_SELF_OUT)
    self_t[...] = shared_rows(ROW_SELF_OUT).T
    for third in range(3):
        piece = shared_rows(ROW_QKV + third, 3)
        qkv_w[:, third * D : (third + 1) * D] = piece
        qkv_t[third * D : (third + 1) * D, :] = piece.T
    for piece_at in range(2 * EXPERTS):
        number, half = piece_at // 2, piece_at % 2
        piece = shared_rows(ROW_UP + number * FF + half, 2)
        up_w[:, piece_at * D : (piece_at + 1) * D] = piece
        up_t[piece_at * D : (piece_at + 1) * D, :] = piece.T
        piece = shared_rows(ROW_DOWN + piece_at * D)
        down_w[piece_at * D : (piece_at + 1) * D, :] = piece
        down_t[:, piece_at * D : (piece_at + 1) * D] = piece.T

    expert_at = lax.broadcasted_iota(jnp.int32, (8, D), 0)
    router_mask = lax.broadcasted_iota(jnp.int32, (8, D), 1) % EXPERTS == expert_at
    turned = jnp.zeros((8, D), F32)
    pickers = []
    for r in range(EXPERTS):
        picker = jnp.where(column_at == r * (D // EXPERTS) + row_at // EXPERTS, 1.0, 0.0).astype(BF16)
        pickers.append(picker)
        router_row = shared_v[ROW_ROUTER + r : ROW_ROUTER + r + 1, :]
        turned = turned + dot(jnp.where(router_mask, router_row, 0.0).astype(BF16), picker)
    router_t[...] = turned.astype(BF16)

    gain_one = to_column(shared_v[ROW_GAIN_ONE : ROW_GAIN_ONE + 1, :])
    bias_one = to_column(shared_v[ROW_BIAS_ONE : ROW_BIAS_ONE + 1, :])
    gain_two = to_column(shared_v[ROW_GAIN_TWO : ROW_GAIN_TWO + 1, :])
    bias_two = to_column(shared_v[ROW_BIAS_TWO : ROW_BIAS_TWO + 1, :])
    gain_three = to_column(shared_v[ROW_GAIN_THREE : ROW_GAIN_THREE + 1, :])
    bias_three = to_column(shared_v[ROW_BIAS_THREE : ROW_BIAS_THREE + 1, :])

    loads[3].wait()

    @pl.loop(0, blocks)
    def first_norm(b):
        points = points_v[span(b), :].astype(F32).T
        after_cross[:, span(b)] = points
        normed, _ = layer_norm(points)
        hidden = (normed * gain_one + bias_one).astype(BF16)
        hidden_one[:, span(b)] = hidden
        cross_soft[:, span(b)] = feature_softmax(dot(query_t[...], hidden))

    exchange(0).wait_recv()
    weight_total = fn_weight + got[0, HEAD_DIM : HEAD_DIM + 1, :]
    fn_share = fn_weight / weight_total
    mixed = unfolded((weighted_summary + got[0, 0:HEAD_DIM, :]) / weight_total)
    mixed_low = mixed.astype(BF16)
    mixed_t = mixed.T.astype(BF16)
    item_count = item_counts[0]

    def usable(b):
        at = lax.broadcasted_iota(jnp.int32, (1, block), 1) + (b * block + fn * rows)
        return at < item_count

    def cross(b, so_far):
        out = dot(mixed_t, cross_soft[:, span(b)].astype(BF16)).astype(BF16)
        cross_out[:, span(b)] = out
        after = after_cross[:, span(b)] + dot(cross_t[...], out)
        after_cross[:, span(b)] = after
        normed, _ = layer_norm(after)
        hidden = (normed * gain_two + bias_two).astype(BF16)
        hidden_two[:, span(b)] = hidden
        qkv = dot(qkv_t[...], hidden)
        self_soft[:, span(b)] = feature_softmax(qkv[:D])
        keys = jnp.where(usable(b), qkv[D : 2 * D], far_below)
        key_powers[:, span(b)] = keys
        self_values[:, span(b)] = qkv[2 * D :].astype(BF16)
        return jnp.maximum(so_far, lane_fold(keys, jnp.maximum))

    key_max = jnp.max(
        lax.fori_loop(0, blocks, cross, jnp.full((D, D), far_below, F32)), axis=1, keepdims=True
    )

    def key_total(b, so_far):
        powers = jnp.where(usable(b), jnp.exp(key_powers[:, span(b)] - key_max), 0.0)
        key_powers[:, span(b)] = powers
        low = powers.astype(BF16)
        key_low[:, span(b)] = low
        return (
            so_far[0] + lane_fold(powers, jnp.add),
            so_far[1] + dot_points(low, self_values[:, span(b)]),
        )

    totals, key_sum = lax.fori_loop(0, blocks, key_total, (nothing, nothing))
    own_total = jnp.sum(totals, axis=1, keepdims=True)
    sent[1, 0:HEAD_DIM, :] = folded(key_sum)
    own_stats = jnp.concatenate([to_row(key_max), to_row(own_total), jnp.zeros((6, D), F32)], axis=0)
    sent[1, HEAD_DIM : HEAD_DIM + 8, :] = own_stats
    exchange(1).start()

    loads[4].wait()
    loads[5].wait()

    @pl.loop(0, blocks)
    def gates(b):
        cot_t[:, span(b)] = cotangent_v[span(b), :].astype(F32).T.astype(BF16)
        logits = dot_points(router_t[...], geometry_v[span(b), :])[:EXPERTS]
        powers = jnp.exp(logits - jnp.max(logits, axis=0, keepdims=True))
        gates_v[0:EXPERTS, span(b)] = powers * (1.0 / jnp.sum(powers, axis=0, keepdims=True))

    zeros(up_sum)
    zeros(down_sum)
    zeros(norm_sums)

    exchange(1).wait_recv()
    other_max = to_column(got[1, HEAD_DIM : HEAD_DIM + 1, :])
    other_total = to_column(got[1, HEAD_DIM + 1 : HEAD_DIM + 2, :])
    joint_max = jnp.maximum(key_max, other_max)
    own_factor, other_factor = jnp.exp(key_max - joint_max), jnp.exp(other_max - joint_max)
    joint_scale = 1.0 / (own_total * own_factor + other_total * other_factor)
    own_factor, other_factor = own_factor * joint_scale, other_factor * joint_scale
    self_summary = diagonal_blocks(key_sum) * own_factor + unfolded(got[1, 0:HEAD_DIM, :]) * other_factor
    self_low = self_summary.astype(BF16)
    self_summary_t = self_summary.T.astype(BF16)

    def experts(b, sums):
        weights = self_soft[:, span(b)].astype(BF16)
        mixed_rows = dot(self_summary_t, weights).astype(BF16)
        self_out_v[:, span(b)] = mixed_rows
        after = after_cross[:, span(b)] + dot(self_t[...], mixed_rows)
        normed, inverse = layer_norm(after)
        hidden = (normed * gain_three + bias_three).astype(BF16)
        arriving = cot_t[:, span(b)]
        gate_grads = []
        for number in range(EXPERTS):
            rows_of = slice(number * FF, (number + 1) * FF)
            gate = gates_v[number : number + 1, span(b)]
            pre = dot(up_t[rows_of, :], hidden)
            back = dot(down_w[rows_of, :], arriving)
            cdf = 0.5 + 0.5 * lax.erf(pre * math.sqrt(0.5))
            density = jnp.exp2(pre * pre * (-0.5 * math.log2(math.e))) * (1.0 / math.sqrt(2.0 * math.pi))
            active = pre * cdf
            gate_grads.append(jnp.sum(active * back, axis=0, keepdims=True))
            hidden_v[rows_of, :] = (active * gate).astype(BF16)
            pre_v[rows_of, :] = (back * gate * (cdf + pre * density)).astype(BF16)
        out_v[span(b), :] = (after + dot(down_t[...], hidden_v[...])).T.astype(BF16)
        down_sum[...] += dot_points(hidden_v[...], arriving)
        up_sum[...] += dot_points(hidden, pre_v[...])
        gate = gates_v[0:EXPERTS, span(b)]
        g_gates = jnp.concatenate(gate_grads, axis=0)
        g_logits = gate * (g_gates - jnp.sum(gate * g_gates, axis=0, keepdims=True))
        g_logits = jnp.concatenate([g_logits, jnp.zeros_like(g_logits)], axis=0).astype(BF16)
        upstream = dot(up_w[...], pre_v[...])
        norm_sums[4] += lane_fold(upstream * normed, jnp.add)
        norm_sums[5] += lane_fold(upstream, jnp.add)
        g_after = arriving.astype(F32) + norm_back(normed, inverse, gain_three, upstream)
        g_self[:, span(b)] = g_after
        g_proj = g_after.astype(BF16)
        g_out = dot(self_w[...], g_proj).astype(BF16)
        g_self_out[:, span(b)] = g_out
        return (
            sums[0] + dot(g_logits, geometry_v[span(b), :]),
            sums[1] + dot_points(mixed_rows, g_proj),
            sums[2] + dot_points(weights, g_out),
        )

    router_sum, self_out_sum, summary_grad = lax.fori_loop(
        0, blocks, experts, (jnp.zeros((8, D), F32), nothing, nothing)
    )
    own_grad = folded(summary_grad)
    sent[2, 0:HEAD_DIM, :] = own_grad
    exchange(2).start()
    for piece_at in range(2 * EXPERTS):
        expert.source[piece_at * D : (piece_at + 1) * D, :] = up_sum[
            :, piece_at * D : (piece_at + 1) * D
        ].astype(BF16)
    expert.source[HIDDEN:, :] = down_sum[...].astype(BF16)
    expert.scatter(0)
    tail.source[T_SELF_OUT : T_SELF_OUT + D, :] = self_out_sum.astype(BF16)

    @pl.loop(0, blocks)
    def query_grads(b):
        back = dot(self_low, g_self_out[:, span(b)])
        g_queries[:, span(b)] = feature_softmax_back(self_soft[:, span(b)], back).astype(BF16)

    exchange(2).wait_recv()
    joint_grad = unfolded(own_grad + got[2, 0:HEAD_DIM, :])
    scaled_grad = joint_grad * own_factor
    correction = jnp.sum(scaled_grad * self_summary, axis=1, keepdims=True)
    scaled_low = scaled_grad.astype(BF16)
    scaled_t = scaled_grad.T.astype(BF16)

    def self_back(b, sums):
        powers = key_powers[:, span(b)]
        g_keys = powers * (dot(scaled_low, self_values[:, span(b)]) - correction)
        g_values = dot(scaled_t, key_low[:, span(b)])
        g_qkv = jnp.concatenate(
            [g_queries[:, span(b)], g_keys.astype(BF16), g_values.astype(BF16)], axis=0
        )
        upstream = dot(qkv_w[...], g_qkv)
        normed, inverse = layer_norm(after_cross[:, span(b)])
        norm_sums[2] += lane_fold(upstream * normed, jnp.add)
        norm_sums[3] += lane_fold(upstream, jnp.add)
        g_after = g_self[:, span(b)] + norm_back(normed, inverse, gain_two, upstream)
        g_cross[:, span(b)] = g_after
        g_proj = g_after.astype(BF16)
        g_out = dot(cross_w[...], g_proj).astype(BF16)
        g_cross_out[:, span(b)] = g_out
        return (
            sums[0] + dot_points(hidden_two[:, span(b)], g_qkv),
            sums[1] + dot_points(cross_out[:, span(b)], g_proj),
            sums[2] + dot_points(cross_soft[:, span(b)].astype(BF16), g_out),
        )

    qkv_sum, cross_out_sum, mixed_grad = lax.fori_loop(
        0, blocks, self_back, (jnp.zeros((D, 3 * D), F32), nothing, nothing)
    )
    own_mixed = folded(mixed_grad)
    sent[3, 0:HEAD_DIM, :] = own_mixed
    exchange(3).start()
    expert.add(0)
    expert.scatter(1)
    for third in range(3):
        tail.source[T_QKV + third * D : T_QKV + (third + 1) * D, :] = qkv_sum[
            :, third * D : (third + 1) * D
        ].astype(BF16)
    tail.source[T_CROSS_OUT : T_CROSS_OUT + D, :] = cross_out_sum.astype(BF16)

    def query_back(b, query_sum):
        g_query = feature_softmax_back(
            cross_soft[:, span(b)], dot(mixed_low, g_cross_out[:, span(b)])
        ).astype(BF16)
        upstream = dot(query_w[...], g_query)
        normed, inverse = layer_norm(points_v[span(b), :].astype(F32).T)
        norm_sums[0] += lane_fold(upstream * normed, jnp.add)
        norm_sums[1] += lane_fold(upstream, jnp.add)
        total = g_cross[:, span(b)] + norm_back(normed, inverse, gain_one, upstream)
        in_grad_v[span(b), :] = total.T.astype(BF16)
        return query_sum + dot_points(hidden_one[:, span(b)], g_query)

    query_sum = lax.fori_loop(0, blocks, query_back, nothing)
    stores = [
        pltpu.make_async_copy(out_v, output_hbm, local_sem.at[6]),
        pltpu.make_async_copy(in_grad_v, input_grad_hbm, local_sem.at[7]),
    ]
    for store in stores:
        store.start()
    tail.source[T_QUERY : T_QUERY + D, :] = query_sum.astype(BF16)
    small = [to_row(jnp.sum(norm_sums[at], axis=1, keepdims=True)) for at in range(6)]
    tail.source[T_SMALL:, :] = jnp.concatenate(
        [router_sum, *small, jnp.zeros((TAIL_ROWS - T_SMALL - 14, D), F32)], axis=0
    ).astype(BF16)
    tail.scatter(0)

    exchange(3).wait_recv()
    fn_grad = unfolded((own_mixed + got[3, 0:HEAD_DIM, :]) * fn_share).astype(BF16).astype(F32)
    fn_scaled = fn_grad * fn_scale
    fn_correction = jnp.sum(fn_scaled * fn_summary, axis=1, keepdims=True)
    fn_scaled_low = fn_scaled.astype(BF16)
    fn_scaled_t = fn_scaled.T.astype(BF16)
    expert.add(1)
    expert.gather(1)

    def branch_back(b, sums):
        g_keys = fn_powers[:, span(b)] * (dot(fn_scaled_low, fn_values[:, span(b)]) - fn_correction)
        g_values = dot(fn_scaled_t, fn_low[:, span(b)])
        g_keyval = jnp.concatenate([g_keys, g_values], axis=0).astype(BF16)
        upstream = dot(kv_w[...], g_keyval)
        normed, _ = layer_norm(functions_v[span(b), :].astype(F32).T)
        return (
            sums[0] + lane_fold(upstream * normed, jnp.add),
            sums[1] + lane_fold(upstream, jnp.add),
            sums[2] + dot_points(fn_hidden[:, span(b)], g_keyval),
        )

    gain_sum, bias_sum, kv_sum = lax.fori_loop(
        0, fn_blocks, branch_back, (nothing, nothing, jnp.zeros((D, 2 * D), F32))
    )
    for half in range(2):
        branch.source[half * D : (half + 1) * D, :] = kv_sum[:, half * D : (half + 1) * D].astype(BF16)
    branch.source[B_SMALL:, :] = jnp.concatenate(
        [
            to_row(jnp.sum(gain_sum, axis=1, keepdims=True)),
            to_row(jnp.sum(bias_sum, axis=1, keepdims=True)),
            jnp.zeros((14, D), F32),
        ],
        axis=0,
    ).astype(BF16)
    branch.scatter(0)

    expert.collect(1)
    expert.gather(0)
    for at in range(len(tail.sizes)):
        tail.add(at)
        if at + 1 < len(tail.sizes):
            tail.scatter(at + 1)
    tail.gather(len(tail.sizes) - 1)
    for at in range(len(branch.sizes)):
        branch.add(at)
        if at + 1 < len(branch.sizes):
            branch.scatter(at + 1)
    branch.gather(len(branch.sizes) - 1)

    expert.collect(0)
    for piece_at in range(2 * EXPERTS):
        number, half = piece_at // 2, piece_at % 2
        shared_out[pl.ds(ROW_UP + number * FF + half, D, stride=2), :] = expert.total[
            piece_at * D : (piece_at + 1) * D, :
        ].astype(F32)
    shared_out[ROW_DOWN : ROW_DOWN + HIDDEN, :] = expert.total[HIDDEN:, :].astype(F32)

    for at in reversed(range(len(tail.sizes))):
        tail.collect(at)
        if at:
            tail.gather(at - 1)
    for at in reversed(range(len(branch.sizes))):
        branch.collect(at)
        if at:
            branch.gather(at - 1)

    def from_tail(start):
        return tail.total[start : start + D, :].astype(F32)

    shared_out[ROW_QUERY : ROW_QUERY + D, :] = from_tail(T_QUERY)
    shared_out[ROW_CROSS_OUT : ROW_CROSS_OUT + D, :] = from_tail(T_CROSS_OUT)
    shared_out[ROW_SELF_OUT : ROW_SELF_OUT + D, :] = from_tail(T_SELF_OUT)
    for third in range(3):
        shared_out[pl.ds(ROW_QKV + third, D, stride=3), :] = from_tail(T_QKV + third * D)
    rest = tail.total[T_SMALL:, :].astype(F32)
    for at, row in enumerate(
        [ROW_GAIN_ONE, ROW_BIAS_ONE, ROW_GAIN_TWO, ROW_BIAS_TWO, ROW_GAIN_THREE, ROW_BIAS_THREE]
    ):
        shared_out[row : row + 1, :] = rest[8 + at : 9 + at]
    router_low = rest[:8].astype(BF16)
    for r in range(EXPERTS):
        spread = dot_points(router_low, pickers[r])
        shared_out[ROW_ROUTER + r : ROW_ROUTER + r + 1, :] = jnp.sum(
            jnp.where(router_mask, spread, 0.0), axis=0, keepdims=True
        )
    for half in range(2):
        branch_out[pl.ds(2 + half, D, stride=2), :] = branch.total[
            half * D : (half + 1) * D, :
        ].astype(F32)
    branch_out[0:2, :] = branch.total[B_SMALL:, :].astype(F32)[0:2]
    stores.append(pltpu.make_async_copy(shared_out, shared_grad_hbm, local_sem.at[8]))
    stores.append(pltpu.make_async_copy(branch_out, branch_grad_hbm, local_sem.at[9]))
    for store in stores[2:]:
        store.start()

    for at in range(4):
        exchange(at).wait_send()
    for reduction in (expert, tail, branch):
        reduction.drain()
    for store in stores:
        store.wait()


def whole_step(fns, pts, points, geometry, functions, presence, fn_counts, item_counts, cotangent, shared, branch):
    rows, fn_rows = points.shape[0], functions.shape[0]
    block = 512
    smem = pl.BlockSpec(memory_space=pltpu.SMEM)
    anywhere = pl.BlockSpec(memory_space=pl.ANY)

    def low(*shape):
        return pltpu.VMEM(shape, BF16)

    def wide(*shape):
        return pltpu.VMEM(shape, F32)

    scratch = [low(rows, D), low(rows, D), low(fn_rows, D), low(rows, D), wide(SHARED_ROWS, D), wide(BRANCH_ROWS, D)]
    scratch += [low(D, D)] * 4 + [low(D, 3 * D), low(3 * D, D)] + [low(D, D)] * 2
    scratch += [low(D, HIDDEN), low(HIDDEN, D), low(HIDDEN, D), low(D, HIDDEN), low(D, 2 * D), low(2 * D, D), low(8, D)]
    scratch += [
        low(D, fn_rows),
        wide(D, fn_rows),
        low(D, fn_rows),
        low(D, fn_rows),
        low(D, rows),
        wide(D, rows),
        low(D, rows),
        wide(D, rows),
        low(D, rows),
        wide(D, rows),
        wide(D, rows),
        low(D, rows),
        low(D, rows),
        low(D, rows),
        low(D, rows),
        wide(8, rows),
        wide(D, rows),
        low(D, rows),
        low(D, rows),
        wide(D, rows),
        low(D, rows),
        low(HIDDEN, block),
        low(HIDDEN, block),
    ]
    scratch += [
        wide(D, HIDDEN),
        wide(HIDDEN, D),
        wide(6, D, D),
        low(rows, D),
        low(rows, D),
        wide(SHARED_ROWS, D),
        wide(BRANCH_ROWS, D),
    ]
    scratch += [wide(4, HEAD_DIM + 8, D), wide(4, HEAD_DIM + 8, D)]
    scratch += [pltpu.SemaphoreType.DMA((10,)), pltpu.SemaphoreType.DMA((4,)), pltpu.SemaphoreType.DMA((4,))]
    for reduction in plan(fns, pts):
        scratch += reduction.scratch()
    return pl.pallas_call(
        functools.partial(step_kernel, fns, pts, block),
        out_shape=[
            jax.ShapeDtypeStruct((rows, D), BF16),
            jax.ShapeDtypeStruct((rows, D), BF16),
            jax.ShapeDtypeStruct((SHARED_ROWS, D), F32),
            jax.ShapeDtypeStruct((BRANCH_ROWS, D), F32),
        ],
        in_specs=[smem] * 3 + [anywhere] * 6,
        out_specs=[anywhere] * 4,
        scratch_shapes=scratch,
        compiler_params=pltpu.CompilerParams(
            collective_id=0, has_side_effects=True, vmem_limit_bytes=56 << 20
        ),
    )(presence, fn_counts, item_counts, points, geometry, functions, cotangent, shared, branch)


def sgd_update(weights, momentum, average, gradient, step_rate):
    momentum_new = momentum_decay * momentum + gradient
    weights_new = weights - step_rate * (gradient + momentum_decay * momentum_new)
    average_new = average_decay * average + (1.0 - average_decay) * weights_new
    return (weights_new, momentum_new, average_new, weights_new.astype(BF16))


def local(
    fns,
    pts,
    points_in,
    geometry,
    functions,
    presence,
    fn_counts,
    item_counts,
    cotangent,
    shared_weights,
    shared_momentum,
    shared_average,
    branch_weights,
    branch_momentum,
    branch_average,
):
    rows, fn_rows = points_in.shape[1], functions.shape[2]
    output, input_grad, shared_total, branch_total = whole_step(
        fns,
        pts,
        points_in.reshape(rows, D),
        geometry.reshape(rows, D),
        functions.reshape(fn_rows, D),
        presence,
        fn_counts,
        item_counts,
        cotangent.reshape(rows, D),
        shared_weights.reshape(SHARED_ROWS, D),
        branch_weights.reshape(BRANCH_ROWS, D),
    )
    norm_grads = jnp.concatenate(
        [
            shared_total[at : at + 2]
            for at in (ROW_GAIN_ONE, ROW_GAIN_TWO, ROW_GAIN_THREE)
        ],
        axis=0,
    )
    shared_rate = 0.1 / math.sqrt(pts * rows * fns)
    branch_rate = 0.1 / math.sqrt(pts * fn_rows)
    shared_new = sgd_update(
        shared_weights, shared_momentum, shared_average, shared_total.reshape(-1), shared_rate
    )
    branch_new = sgd_update(
        branch_weights, branch_momentum, branch_average, branch_total.reshape(1, -1), branch_rate
    )
    return (
        output.reshape(1, rows, D),
        input_grad.reshape(1, rows, D),
        *shared_new,
        *branch_new,
        norm_grads,
    )


def solution(mesh):
    split = P("pts", "fn", None)
    return jax.shard_map(
        functools.partial(local, mesh.shape["fn"], mesh.shape["pts"]),
        mesh=mesh,
        in_specs=(
            split,
            split,
            P("fn", "pts", None, None),
            P("fn", "pts"),
            P("fn", "pts"),
            P("pts"),
            split,
            P(),
            P(),
            P(),
            P("fn", None),
            P("fn", None),
            P("fn", None),
        ),
        out_specs=(
            split,
            split,
            P(),
            P(),
            P(),
            P(),
            P("fn", None),
            P("fn", None),
            P("fn", None),
            P("fn", None),
            P(),
        ),
        check_vma=False,
    )
```

time: 432 us -> 82.8 us (0.19); the launches traced: 424 us -> 82 us
  waiting for transfers between devices: 173 us -> 0 us
  Pallas kernels: 0 us -> 66.8 us
  local copies, waits for them, and re-layouts: 63.9 us -> 2.51 us
  matrix products: 54 us -> 0 us
  other arithmetic: 63.6 us -> 10 us
  blocking collectives: 49.9 us -> 0 us
  between operations: 18.7 us -> 2.63 us
    psum x2 -> x0, waiting for transfers between devices: 173 us -> none  [the longest x1 136 us: local(): lax.psum(jnp.concatenate([front_grad, back_grad]), ('fn', 'pts'))]
    pallas_call x0 -> x1, Pallas kernels: none -> 66.8 us  [whole_step(): pl.pallas_call(functools.partial(step_kernel, fns, pts, block), out_shape...]
    dot_general x35 -> x0, matrix products: 54 us -> none  [the longest x4 6.75 us: apply_transposed(): jnp.einsum('inhe,ihje->inhj', heads_view(gradients), summary, preferred_e...]
    psum x5 -> x0, blocking collectives: 41.5 us -> none  [the longest x1 12 us: local(): mixed_total = lax.psum(weighted_summary, 'fn')]
    unnamed x256 -> x22, local copies, waits for them, and re-layouts: 40.7 us -> 1.82 us
    convert_element_type x8 -> x2, other arithmetic: 30.8 us -> 5.28 us  [sgd_update(): return (weights_new, momentum_new, average_new, weights_new.astype(BF16))]
    reduce_sum x19 -> x0, other arithmetic: 14.6 us -> none  [the longest x5 5.99 us: layer_norm(): return centred * lax.rsqrt(spread + epsilon) * norm_gain + norm_bias]
    all_gather x2 -> x0, blocking collectives: 8.42 us -> none  [merged(): pieces = jax.tree.map(lambda part: lax.all_gather(part, axis), value)]
  transfers between devices with their start and end apart: 2 -> 0, of which waited for: 2 -> 0; matrix products, arithmetic and copies ran while one was open for 13% -> 0% of each run, Pallas kernels for 0% -> 0%
where the time goes in v1:
time: 82.8 us; the launch traced here: 82 us
  Pallas kernels  66.8 us (81%)
  other arithmetic  10 us (12%)
  between operations  2.63 us (3%)
  local copies, waits for them, and re-layouts  2.51 us (3%)
    pallas_call x1, Pallas kernels, whole_step(): pl.pallas_call(functools.partial(step_kernel, fns, pts, block), out_shape...  66.8 us
    convert_element_type x2, other arithmetic, sgd_update(): return (weights_new, momentum_new, average_new, weights_new.astype(BF16))  5.28 us
    add x2, other arithmetic, sgd_update(): average_new = average_decay * average + (1.0 - average_decay) * weights_new  2.24 us
    unnamed x1, other arithmetic  1.88 us
    unnamed x22, local copies, waits for them, and re-layouts  1.82 us

profile of v1, /device:TPU:0, one launch (start us, length us, event | category | flops | bytes accessed | tf_op | source)
XLA Modules:
  0.0 82.0 jit_solution(4507167729183571949)
XLA Ops:
  2.6 1.9 %reduce = f32[33024]{0:T(1024)} reduce(f32[1,33024]{1,0:T(1,128)} %param.23, f32[]{:T(128)} %constant.23), dimensions={0}, to_apply=%param.23.reduce_sub_computation | reduce | bytes 264196 | tf_op args[10]
  4.5 0.0 copy-start.4
  4.5 0.0 copy-start.8
  4.5 0.0 copy-start.9
  4.5 0.0 copy-start
  4.5 0.0 copy-start.2
  4.5 66.8 %shard_map.212 = (bf16[2048,128]{1,0:T(8,128)(2,1)}, bf16[2048,128]{1,0:T(8,128)(2,1)}, f32[2826,128]{1,0:T(8,128)}, f32[258,128]{1,0:T(8,128)}) custom-call(s32[1,1]{1,0:T(1,128)S(6)} %copy.31.refs_0_, s32[1,1]{1,0:T(1,128)S(6)} %copy.32.refs_1_, s32[1]{0:T(128)S(6)} %copy.33.refs_2_, bf16[2048,128]{1,0:T(8,128)(2,1)} %bitcast.30, ...), custom_call_target="tpu_custom_call" | custom-call | tf_op jit(solution)/shard_map/pallas_call | solution.py:891
  71.3 0.7 fusion.8
  72.0 0.6 pad_maximum_fusion
  72.6 0.0 copy-done.4
  72.6 0.0 copy-done.8
  72.6 2.1 %fusion.4 = (bf16[1,33024]{1,0:T(2,128)(2,1)}, f32[1,33024]{1,0:T(1,128)S(1)}, f32[1,33024]{1,0:T(1,128)}) fusion(f32[1,33024]{1,0:T(1,128)S(1)} %copy-done.4, f32[1,1,258,128]{3,2,1,0:T(8,128)} %bitcast.36, f32[1,33024]{1,0:T(1,128)S(1)} %copy-done.8), kind=kLoop, calls=%fused_computation.11 | loop fusion | flops 231168 | bytes 726528 | tf_op jit(solution)/shard_map/convert_element_type | solution.py:912
  74.7 0.0 copy-start.5
  74.7 0.0 copy-done.9
  74.7 0.9 %multiply_add_fusion.1 = f32[1,33024]{1,0:T(1,128)} fusion(f32[1,33024]{1,0:T(1,128)S(1)} %get-tuple-element.45, f32[1,33024]{1,0:T(1,128)S(1)} %copy-done.9), kind=kLoop, calls=%fused_computation.9 | loop fusion | flops 99072 | bytes 396288 | tf_op jit(solution)/shard_map/add | solution.py:911
  75.6 0.0 copy-done
  75.6 0.0 copy-done.2
  75.6 0.0 copy-start.3
  75.6 3.2 %fusion.6 = (bf16[361728]{0:T(1024)(128)(2,1)}, f32[361728]{0:T(1024)S(1)}, f32[361728]{0:T(1024)}) fusion(f32[361728]{0:T(1024)S(1)} %copy-done, f32[2826,128]{1,0:T(8,128)} %get-tuple-element.17, f32[361728]{0:T(1024)S(1)} %copy-done.2), kind=kLoop, calls=%fused_computation.12 | loop fusion | flops 2532096 | bytes 7958016 | tf_op jit(solution)/shard_map/convert_element_type | solution.py:912
  78.8 0.0 copy-done.5
  78.8 0.0 copy-start.1
  78.8 0.0 copy-done.3
  78.8 0.0 copy-start.7
  78.8 0.0 copy-start.6
  78.8 1.4 %multiply_add_fusion = f32[361728]{0:T(1024)} fusion(f32[361728]{0:T(1024)S(1)} %get-tuple-element.41, f32[361728]{0:T(1024)S(1)} %copy-done.3), kind=kLoop, calls=%fused_computation.4 | loop fusion | flops 1085184 | bytes 4340736 | tf_op jit(solution)/shard_map/add | solution.py:911
  80.2 0.2 copy-done.1
  80.4 0.0 copy-done.7
  80.4 0.8 copy.34
  81.2 0.0 copy-done.6
  81.2 0.8 copy.35
Async XLA Ops:
  4.5 68.1 %copy-start.4 = (f32[1,33024]{1,0:T(1,128)S(1)}, f32[1,33024]{1,0:T(1,128)}, u32[]{:S(2)}) copy-start(f32[1,33024]{1,0:T(1,128)} %param.23) | copy-start | bytes 396292
  4.5 68.1 %copy-start.8 = (f32[1,33024]{1,0:T(1,128)S(1)}, f32[1,33024]{1,0:T(1,128)}, u32[]{:S(2)}) copy-start(f32[1,33024]{1,0:T(1,128)} %param.24) | copy-start | bytes 396292
  4.5 70.2 %copy-start.9 = (f32[1,33024]{1,0:T(1,128)S(1)}, f32[1,33024]{1,0:T(1,128)}, u32[]{:S(2)}) copy-start(f32[1,33024]{1,0:T(1,128)} %param.25) | copy-start | bytes 396292
  4.5 71.1 %copy-start = (f32[361728]{0:T(1024)S(1)}, f32[361728]{0:T(1024)}, u32[]{:S(2)}) copy-start(f32[361728]{0:T(1024)} %param.20) | copy-start | bytes 4340740
  4.5 71.1 %copy-start.2 = (f32[361728]{0:T(1024)S(1)}, f32[361728]{0:T(1024)}, u32[]{:S(2)}) copy-start(f32[361728]{0:T(1024)} %param.21) | copy-start | bytes 4340740
  74.7 4.1 %copy-start.5 = (f32[1,33024]{1,0:T(1,128)}, f32[1,33024]{1,0:T(1,128)S(1)}, u32[]{:S(2)}) copy-start(f32[1,33024]{1,0:T(1,128)S(1)} %get-tuple-element.45) | copy-start | bytes 396292
  75.6 3.2 %copy-start.3 = (f32[361728]{0:T(1024)S(1)}, f32[361728]{0:T(1024)}, u32[]{:S(2)}) copy-start(f32[361728]{0:T(1024)} %param.22) | copy-start | bytes 4340740
  78.8 1.6 %copy-start.1 = (f32[361728]{0:T(1024)}, f32[361728]{0:T(1024)S(1)}, u32[]{:S(2)}) copy-start(f32[361728]{0:T(1024)S(1)} %get-tuple-element.41) | copy-start | bytes 4340740
  78.8 1.6 %copy-start.7 = (bf16[2048,128]{1,0:T(8,128)(2,1)S(1)}, bf16[2048,128]{1,0:T(8,128)(2,1)}, u32[]{:S(2)}) copy-start(bf16[2048,128]{1,0:T(8,128)(2,1)} %get-tuple-element.15) | copy-start | bytes 1572868
  78.8 2.4 %copy-start.6 = (bf16[2048,128]{1,0:T(8,128)(2,1)S(1)}, bf16[2048,128]{1,0:T(8,128)(2,1)}, u32[]{:S(2)}) copy-start(bf16[2048,128]{1,0:T(8,128)(2,1)} %get-tuple-element.16) | copy-start | bytes 1572868

commit v2 on v1

v2 whole, which is shorter than its diff:
```python
import functools
import math

import jax
import jax.numpy as jnp
from jax import lax
from jax.experimental import pallas as pl
from jax.experimental.pallas import tpu as pltpu
from jax.sharding import PartitionSpec as P

D = 128
HEADS = 8
FF = 256
EXPERTS = 4
HEAD_DIM = 16
HIDDEN = EXPERTS * FF

epsilon = 1e-05
far_below = -1e30
momentum_decay = 0.9
average_decay = 0.95

F32 = jnp.float32
BF16 = jnp.bfloat16
MESH = pl.DeviceIdType.MESH

ROW_GAIN_ONE, ROW_BIAS_ONE = 0, 1
ROW_QUERY = 2
ROW_CROSS_OUT = ROW_QUERY + D
ROW_GAIN_TWO = ROW_CROSS_OUT + D
ROW_BIAS_TWO = ROW_GAIN_TWO + 1
ROW_QKV = ROW_BIAS_TWO + 1
ROW_SELF_OUT = ROW_QKV + 3 * D
ROW_GAIN_THREE = ROW_SELF_OUT + D
ROW_BIAS_THREE = ROW_GAIN_THREE + 1
ROW_ROUTER = ROW_BIAS_THREE + 1
ROW_UP = ROW_ROUTER + EXPERTS
ROW_DOWN = ROW_UP + 2 * D * EXPERTS
SHARED_ROWS = ROW_DOWN + HIDDEN
BRANCH_ROWS = 2 + 2 * D

EXPERT_ROWS = 2 * FF
MIDDLE_ROWS = 4 * D
LAST_ROWS = 2 * D + 32
BRANCH_SENT = 2 * D


def dot(a, b):
    return jnp.dot(a, b, preferred_element_type=F32)


def dot_points(a, b):
    return lax.dot_general(a, b, (((1,), (1,)), ((), ())), preferred_element_type=F32)


class Level:
    def __init__(self, size, index, member):
        self.size, self.index, self.member = size, index, member


def split_rows(rows, size):
    step = 16
    while rows % step or rows // step > size:
        step += 16
    return step, rows // step


class Reduction:
    def __init__(self, sizes, rows):
        self.sizes, self.rows = sizes, rows
        self.steps, self.owners = [], []
        for size in sizes:
            step, owners = split_rows(rows, size)
            self.steps.append(step)
            self.owners.append(owners)
            rows = step

    def scratch(self):
        shapes = [pltpu.VMEM((self.rows, D), BF16), pltpu.VMEM((self.rows, D), BF16)]
        for at, size in enumerate(self.sizes):
            shapes.append(pltpu.VMEM(((size - 1) * self.steps[at], D), BF16))
            shapes.append(pltpu.VMEM((self.steps[at], D), BF16))
            shapes.append(pltpu.SemaphoreType.DMA((4,)))
        return shapes

    def bind(self, refs, levels):
        self.source, self.total = refs[0], refs[1]
        self.parts = [refs[2 + 3 * at : 5 + 3 * at] for at in range(len(self.sizes))]
        self.levels = levels
        last = len(self.sizes) - 1
        self.steps_left = []
        for at in range(last):
            self.steps_left.append(lambda at=at: (self.add(at), self.scatter(at + 1)))
        self.steps_left.append(lambda: (self.add(last), self.gather(last)))
        for at in range(last, 0, -1):
            self.steps_left.append(lambda at=at: (self.collect(at), self.gather(at - 1)))
        self.steps_left.append(lambda: self.collect(0))

    def begin(self):
        self.scatter(0)

    def advance(self):
        if self.steps_left:
            self.steps_left.pop(0)()

    def base(self, at):
        start = 0
        for upper in range(at):
            start = start + self.levels[upper].index * self.steps[upper]
        return start

    def inside(self, at):
        condition = None
        for upper in range(at):
            if self.owners[upper] < self.sizes[upper]:
                here = self.levels[upper].index < self.owners[upper]
                condition = here if condition is None else jnp.logical_and(condition, here)
        return condition

    def when(self, condition, body):
        if condition is None:
            body()
        else:
            pl.when(condition)(body)

    def split(self, at, owner, other):
        def go():
            if self.owners[at] == self.sizes[at]:
                owner()
            else:
                here = self.levels[at].index < self.owners[at]
                pl.when(here)(owner)
                if other is not None:
                    pl.when(jnp.logical_not(here))(other)

        self.when(self.inside(at), go)

    def rows_from(self, at):
        return self.source if at == 0 else self.parts[at - 1][1]

    def wait(self, at, sem, rows, sending):
        window = self.source if rows <= self.rows else self.parts[at][0]
        copy = pltpu.make_async_remote_copy(
            src_ref=window.at[pl.ds(0, rows), :],
            dst_ref=window.at[pl.ds(0, rows), :],
            send_sem=self.parts[at][2].at[sem],
            recv_sem=self.parts[at][2].at[sem],
            device_id=self.levels[at].member(self.levels[at].index),
            device_id_type=MESH,
        )
        (copy.wait_send if sending else copy.wait_recv)()

    def scatter(self, at):
        level, step, owners = self.levels[at], self.steps[at], self.owners[at]
        received, _, sems = self.parts[at]

        def go():
            def one(k, carry):
                peer = (level.index + k) % level.size

                def start():
                    pltpu.make_async_remote_copy(
                        src_ref=self.rows_from(at).at[pl.ds(pl.multiple_of(peer * step, 16), step), :],
                        dst_ref=received.at[pl.ds(pl.multiple_of((k - 1) * step, 16), step), :],
                        send_sem=sems.at[0],
                        recv_sem=sems.at[1],
                        device_id=level.member(peer),
                        device_id_type=MESH,
                    ).start()

                self.when(None if owners == level.size else peer < owners, start)
                return carry

            lax.fori_loop(1, level.size, one, 0)

        self.when(self.inside(at), go)

    def add(self, at):
        level, step = self.levels[at], self.steps[at]

        def go():
            received, kept, _ = self.parts[at]
            self.wait(at, 1, (level.size - 1) * step, False)
            start = pl.multiple_of(level.index * step, 16)
            total = self.rows_from(at)[pl.ds(start, step), :].astype(F32)
            for k in range(level.size - 1):
                total = total + received[k * step : (k + 1) * step, :].astype(F32)
            if at + 1 < len(self.sizes):
                kept[...] = total.astype(BF16)
            else:
                self.total[pl.ds(pl.multiple_of(self.base(at) + start, 16), step), :] = total.astype(BF16)

        self.split(at, go, None)

    def gather(self, at):
        level, step = self.levels[at], self.steps[at]
        sems = self.parts[at][2]

        def go():
            rows = pl.ds(pl.multiple_of(self.base(at) + level.index * step, 16), step)

            def one(k, carry):
                pltpu.make_async_remote_copy(
                    src_ref=self.total.at[rows, :],
                    dst_ref=self.total.at[rows, :],
                    send_sem=sems.at[2],
                    recv_sem=sems.at[3],
                    device_id=level.member((level.index + k) % level.size),
                    device_id_type=MESH,
                ).start()
                return carry

            lax.fori_loop(1, level.size, one, 0)

        self.split(at, go, None)

    def collect(self, at):
        step, owners = self.steps[at], self.owners[at]
        self.split(
            at,
            lambda: self.wait(at, 3, (owners - 1) * step, False) if owners > 1 else None,
            lambda: self.wait(at, 3, owners * step, False),
        )

    def drain(self):
        for at, size in enumerate(self.sizes):
            step, owners = self.steps[at], self.owners[at]

            def owner():
                if owners > 1:
                    self.wait(at, 0, (owners - 1) * step, True)
                self.wait(at, 2, (size - 1) * step, True)

            self.split(at, owner, lambda: self.wait(at, 0, owners * step, True))


def inner_size(pts):
    return 2 if pts % 2 == 0 else 1


def plan(fns, pts):
    core = inner_size(pts)
    outer = pts // core
    if fns * outer <= 16:
        everyone, items = [core, fns * outer], [core, outer]
    else:
        everyone, items = [core, fns * 4, outer // 4], [core, 4, outer // 4]
    return [Reduction(everyone, EXPERT_ROWS) for _ in range(EXPERTS)] + [
        Reduction(everyone, MIDDLE_ROWS),
        Reduction(everyone, LAST_ROWS),
        Reduction(items, BRANCH_SENT),
    ]


def layer_norm(values):
    centred = values - jnp.mean(values, axis=0, keepdims=True)
    spread = jnp.mean(centred * centred, axis=0, keepdims=True)
    inverse = lax.rsqrt(spread + epsilon)
    return centred * inverse, inverse


def norm_back(normed, inverse, gain, upstream):
    scaled = upstream * gain
    first = jnp.mean(scaled, axis=0, keepdims=True)
    second = jnp.mean(scaled * normed, axis=0, keepdims=True)
    return (scaled - first - normed * second) * inverse


def heads_view(values):
    return values.reshape(HEADS, HEAD_DIM, values.shape[-1])


def feature_softmax(values):
    shaped = heads_view(values)
    powers = jnp.exp(shaped - jnp.max(shaped, axis=1, keepdims=True))
    return (powers * (1.0 / jnp.sum(powers, axis=1, keepdims=True))).reshape(values.shape)


def feature_softmax_back(soft, upstream):
    shaped, incoming = heads_view(soft), heads_view(upstream)
    inner = jnp.sum(shaped * incoming, axis=1, keepdims=True)
    return (shaped * (incoming - inner)).reshape(soft.shape)


def over_points(values):
    return jnp.sum(values, axis=1, keepdims=True)


def step_kernel(fns, pts, *refs):
    refs = list(refs)

    def take(n):
        got = refs[:n]
        del refs[:n]
        return got

    presence, fn_counts, item_counts = take(3)
    points_hbm, geometry_hbm, functions_hbm, cotangent_hbm, shared_hbm, branch_hbm = take(6)
    output, input_grad, shared_out, branch_out = take(4)
    points_v, geometry_v, functions_v, cotangent_v, shared_v, branch_v, branch_rows = take(7)
    fn_powers, fn_low, fn_values, fn_hidden, hidden_v, pre_v = take(6)
    sent, got = take(2)
    local_sem, x_send, x_recv = take(3)
    reductions = plan(fns, pts)
    bound = [take(len(reduction.scratch())) for reduction in reductions]
    assert not refs

    fn, pt = lax.axis_index("fn"), lax.axis_index("pts")
    core_size = inner_size(pts)
    outer_size = pts // core_size
    outer, core = pt // core_size, pt % core_size
    core_level = Level(core_size, core, lambda j: (fn, outer * core_size + j))
    if fns * outer_size <= 16:
        everyone = [
            core_level,
            Level(
                fns * outer_size,
                fn * outer_size + outer,
                lambda j: (j // outer_size, j % outer_size * core_size + core),
            ),
        ]
        items = [core_level, Level(outer_size, outer, lambda j: (fn, j * core_size + core))]
        greeted = everyone
    else:
        far, near = outer // 4, outer % 4
        far_level = Level(outer_size // 4, far, lambda j: (fn, (j * 4 + near) * core_size + core))
        everyone = [
            core_level,
            Level(fns * 4, fn * 4 + near, lambda j: (j // 4, (far * 4 + j % 4) * core_size + core)),
            far_level,
        ]
        items = [core_level, Level(4, near, lambda j: (fn, (far * 4 + j) * core_size + core)), far_level]
        greeted = everyone
    for reduction, scratch in zip(reductions, bound):
        reduction.bind(scratch, items if reduction is reductions[-1] else everyone)
    experts, middle, last, branch = reductions[:EXPERTS], *reductions[EXPERTS:]

    rows, fn_rows = points_v.shape[0], functions_v.shape[0]

    loads = []
    for at, (source, target) in enumerate(
        [
            (branch_hbm, branch_v),
            (functions_hbm, functions_v),
            (shared_hbm, shared_v),
            (points_hbm, points_v),
            (geometry_hbm, geometry_v),
            (cotangent_hbm, cotangent_v),
        ]
    ):
        loads.append(pltpu.make_async_copy(source, target, local_sem.at[at]))
        loads[-1].start()

    barrier = pltpu.get_barrier_semaphore()
    for level in greeted:

        def greet(k, carry, level=level):
            pl.semaphore_signal(
                barrier,
                inc=1,
                device_id=level.member((level.index + k) % level.size),
                device_id_type=MESH,
            )
            return carry

        lax.fori_loop(1, level.size, greet, 0)

    def exchange(at):
        return pltpu.make_async_remote_copy(
            src_ref=sent.at[at],
            dst_ref=got.at[at],
            send_sem=x_send.at[at],
            recv_sem=x_recv.at[at],
            device_id=((fn + 1) % fns, pt),
            device_id_type=MESH,
        )

    row_at = lax.broadcasted_iota(jnp.int32, (D, D), 0)
    column_at = lax.broadcasted_iota(jnp.int32, (D, D), 1)
    same_head = row_at // HEAD_DIM == column_at // HEAD_DIM
    diagonal = row_at == column_at

    def diagonal_blocks(full):
        return jnp.where(same_head, full, 0.0)

    def folded(full):
        kept = diagonal_blocks(full)
        out = kept[:HEAD_DIM]
        for head in range(1, HEADS):
            out = out + kept[head * HEAD_DIM : (head + 1) * HEAD_DIM]
        return out

    def unfolded(compact):
        return diagonal_blocks(jnp.concatenate([compact] * HEADS, axis=0))

    def to_row(column):
        return jnp.sum(jnp.where(diagonal, column, 0.0), axis=0, keepdims=True)

    def to_column(row):
        return jnp.sum(jnp.where(diagonal, row, 0.0), axis=1, keepdims=True)

    loads[0].wait()
    for r in range(BRANCH_ROWS):
        branch_rows[r : r + 1, :] = branch_v[0:1, r * D : (r + 1) * D]
    kv = jnp.concatenate(
        [branch_rows[pl.ds(2, D, stride=2), :], branch_rows[pl.ds(3, D, stride=2), :]], axis=1
    ).astype(BF16)
    branch_gain = to_column(branch_rows[0:1, :])
    branch_bias = to_column(branch_rows[1:2, :])
    fn_count = fn_counts[0, 0]
    fn_weight = (presence[0, 0] * fn_count).astype(F32)
    fn_usable = lax.broadcasted_iota(jnp.int32, (1, fn_rows), 1) < fn_count
    loads[1].wait()
    normed, _ = layer_norm(functions_v[...].astype(F32).T)
    hidden = (normed * branch_gain + branch_bias).astype(BF16)
    fn_hidden[...] = hidden
    keyval = dot(kv.T, hidden)
    keys = jnp.where(fn_usable, keyval[:D], far_below)
    fn_values[...] = keyval[D:].astype(BF16)
    fn_max = jnp.max(keys, axis=1, keepdims=True)
    powers = jnp.where(fn_usable, jnp.exp(keys - fn_max), 0.0)
    fn_powers[...] = powers
    fn_low[...] = powers.astype(BF16)
    fn_scale = 1.0 / over_points(powers)
    fn_summary = diagonal_blocks(dot_points(fn_low[...], fn_values[...]) * fn_scale)
    weighted_summary = fn_weight * folded(fn_summary)
    sent[0, 0:HEAD_DIM, :] = weighted_summary
    sent[0, HEAD_DIM : HEAD_DIM + 8, :] = jnp.full((8, D), fn_weight, F32)
    pl.semaphore_wait(barrier, sum(level.size - 1 for level in greeted))
    exchange(0).start()

    loads[2].wait()

    def shared_rows(start, stride=1):
        return shared_v[pl.ds(start, D, stride=stride), :].astype(BF16)

    query_w = shared_rows(ROW_QUERY)
    cross_w = shared_rows(ROW_CROSS_OUT)
    self_w = shared_rows(ROW_SELF_OUT)
    qkv_w = jnp.concatenate([shared_rows(ROW_QKV + third, 3) for third in range(3)], axis=1)

    expert_at = lax.broadcasted_iota(jnp.int32, (8, D), 0)
    router_mask = lax.broadcasted_iota(jnp.int32, (8, D), 1) % EXPERTS == expert_at
    router_t = jnp.zeros((8, D), F32)
    pickers = []
    for r in range(EXPERTS):
        picker = jnp.where(column_at == r * (D // EXPERTS) + row_at // EXPERTS, 1.0, 0.0).astype(BF16)
        pickers.append(picker)
        router_row = shared_v[ROW_ROUTER + r : ROW_ROUTER + r + 1, :]
        router_t = router_t + dot(jnp.where(router_mask, router_row, 0.0).astype(BF16), picker)
    router_t = router_t.astype(BF16)

    def shared_column(row):
        return to_column(shared_v[row : row + 1, :])

    gain_one, bias_one = shared_column(ROW_GAIN_ONE), shared_column(ROW_BIAS_ONE)
    gain_two, bias_two = shared_column(ROW_GAIN_TWO), shared_column(ROW_BIAS_TWO)
    gain_three, bias_three = shared_column(ROW_GAIN_THREE), shared_column(ROW_BIAS_THREE)

    loads[3].wait()
    points = points_v[...].astype(F32).T
    normed_one, inverse_one = layer_norm(points)
    hidden_one = (normed_one * gain_one + bias_one).astype(BF16)
    cross_soft = feature_softmax(dot(query_w.T, hidden_one))
    cross_low = cross_soft.astype(BF16)

    exchange(0).wait_recv()
    weight_total = fn_weight + got[0, HEAD_DIM : HEAD_DIM + 1, :]
    fn_share = fn_weight / weight_total
    mixed = unfolded((weighted_summary + got[0, 0:HEAD_DIM, :]) / weight_total)
    mixed_low = mixed.astype(BF16)
    cross_out = dot(mixed.T.astype(BF16), cross_low).astype(BF16)
    after_cross = points + dot(cross_w.T, cross_out)
    normed_two, inverse_two = layer_norm(after_cross)
    hidden_two = (normed_two * gain_two + bias_two).astype(BF16)
    qkv = dot(qkv_w.T, hidden_two)
    usable = lax.broadcasted_iota(jnp.int32, (1, rows), 1) + fn * rows < item_counts[0]
    keys = jnp.where(usable, qkv[D : 2 * D], far_below)
    self_values = qkv[2 * D :].astype(BF16)
    key_max = jnp.max(keys, axis=1, keepdims=True)
    key_powers = jnp.where(usable, jnp.exp(keys - key_max), 0.0)
    key_low = key_powers.astype(BF16)
    own_total = over_points(key_powers)
    key_sum = dot_points(key_low, self_values)
    sent[1, 0:HEAD_DIM, :] = folded(key_sum)
    sent[1, HEAD_DIM : HEAD_DIM + 8, :] = jnp.concatenate(
        [to_row(key_max), to_row(own_total), jnp.zeros((6, D), F32)], axis=0
    )
    exchange(1).start()

    self_soft = feature_softmax(qkv[:D])
    self_weights = self_soft.astype(BF16)
    loads[4].wait()
    logits = dot_points(router_t, geometry_v[...])[:EXPERTS]
    powers = jnp.exp(logits - jnp.max(logits, axis=0, keepdims=True))
    gates = powers * (1.0 / jnp.sum(powers, axis=0, keepdims=True))
    half_gates = 0.5 * gates
    loads[5].wait()
    arriving = cotangent_v[...].astype(F32).T
    arriving_low = arriving.astype(BF16)

    exchange(1).wait_recv()
    other_max = to_column(got[1, HEAD_DIM : HEAD_DIM + 1, :])
    other_total = to_column(got[1, HEAD_DIM + 1 : HEAD_DIM + 2, :])
    joint_max = jnp.maximum(key_max, other_max)
    own_factor, other_factor = jnp.exp(key_max - joint_max), jnp.exp(other_max - joint_max)
    joint_scale = 1.0 / (own_total * own_factor + other_total * other_factor)
    own_factor, other_factor = own_factor * joint_scale, other_factor * joint_scale
    self_summary = diagonal_blocks(key_sum) * own_factor + unfolded(got[1, 0:HEAD_DIM, :]) * other_factor
    self_low = self_summary.astype(BF16)

    self_out = dot(self_summary.T.astype(BF16), self_weights).astype(BF16)
    after_self = after_cross + dot(self_w.T, self_out)
    normed_three, inverse_three = layer_norm(after_self)
    hidden_three = (normed_three * gain_three + bias_three).astype(BF16)

    result, upstream, gate_grads = after_self, None, []
    for number in range(EXPERTS):
        up = jnp.concatenate([shared_rows(ROW_UP + number * FF + half, 2) for half in range(2)], axis=1)
        down = jnp.concatenate(
            [shared_rows(ROW_DOWN + number * FF + half * D) for half in range(2)], axis=0
        )
        gate = half_gates[number : number + 1]
        argument = dot(up.T, hidden_three)
        back = dot(down, arriving_low)
        scaled = argument * math.sqrt(0.5)
        twice_cdf = 1.0 + lax.erf(scaled)
        bell = jnp.exp2(scaled * scaled * -math.log2(math.e)) * (2.0 / math.sqrt(math.pi))
        active = argument * twice_cdf
        gate_grads.append(0.5 * jnp.sum(active * back, axis=0, keepdims=True))
        hidden_v[...] = (active * gate).astype(BF16)
        pre_v[...] = (back * gate * (twice_cdf + scaled * bell)).astype(BF16)
        result = result + dot(down.T, hidden_v[...])
        part = dot(up, pre_v[...])
        upstream = part if upstream is None else upstream + part
        sums = experts[number]
        up_sum = dot_points(hidden_three, pre_v[...])
        sums.source[0:D, :] = up_sum[:, :D].astype(BF16)
        sums.source[D : 2 * D, :] = up_sum[:, D:].astype(BF16)
        sums.source[FF:, :] = dot_points(hidden_v[...], arriving_low).astype(BF16)
        sums.begin()
        for earlier in experts[:number]:
            earlier.advance()
    output[...] = result.T.astype(BF16)

    gate_grads = jnp.concatenate(gate_grads, axis=0)
    g_logits = gates * (gate_grads - jnp.sum(gates * gate_grads, axis=0, keepdims=True))
    g_logits = jnp.concatenate([g_logits, jnp.zeros_like(g_logits)], axis=0).astype(BF16)
    router_sum = dot(g_logits, geometry_v[...])
    small = [None] * 6
    small[4] = to_row(over_points(upstream * normed_three))
    small[5] = to_row(over_points(upstream))
    g_after_self = arriving + norm_back(normed_three, inverse_three, gain_three, upstream)
    g_proj = g_after_self.astype(BF16)
    g_self_out = dot(self_w, g_proj).astype(BF16)
    own_grad = folded(dot_points(self_weights, g_self_out))
    sent[2, 0:HEAD_DIM, :] = own_grad
    exchange(2).start()
    for earlier in experts:
        earlier.advance()
    last.source[D : 2 * D, :] = dot_points(self_out, g_proj).astype(BF16)
    g_queries = feature_softmax_back(self_soft, dot(self_low, g_self_out)).astype(BF16)

    exchange(2).wait_recv()
    scaled_grad = unfolded(own_grad + got[2, 0:HEAD_DIM, :]) * own_factor
    correction = over_points(scaled_grad * self_summary)
    g_keys = key_powers * (dot(scaled_grad.astype(BF16), self_values) - correction)
    g_values = dot(scaled_grad.T.astype(BF16), key_low)
    g_qkv = jnp.concatenate([g_queries, g_keys.astype(BF16), g_values.astype(BF16)], axis=0)
    upstream = dot(qkv_w, g_qkv)
    small[2] = to_row(over_points(upstream * normed_two))
    small[3] = to_row(over_points(upstream))
    g_after_cross = g_after_self + norm_back(normed_two, inverse_two, gain_two, upstream)
    g_proj = g_after_cross.astype(BF16)
    g_cross_out = dot(cross_w, g_proj).astype(BF16)
    own_mixed = folded(dot_points(cross_low, g_cross_out))
    sent[3, 0:HEAD_DIM, :] = own_mixed
    exchange(3).start()
    qkv_sum = dot_points(hidden_two, g_qkv)
    for third in range(3):
        middle.source[third * D : (third + 1) * D, :] = qkv_sum[:, third * D : (third + 1) * D].astype(BF16)
    middle.source[3 * D :, :] = dot_points(cross_out, g_proj).astype(BF16)
    middle.begin()
    for earlier in experts:
        earlier.advance()

    g_query = feature_softmax_back(cross_soft, dot(mixed_low, g_cross_out)).astype(BF16)
    upstream = dot(query_w, g_query)
    small[0] = to_row(over_points(upstream * normed_one))
    small[1] = to_row(over_points(upstream))
    total = g_after_cross + norm_back(normed_one, inverse_one, gain_one, upstream)
    input_grad[...] = total.T.astype(BF16)
    last.source[0:D, :] = dot_points(hidden_one, g_query).astype(BF16)
    for earlier in [middle, *experts]:
        earlier.advance()

    exchange(3).wait_recv()
    fn_grad = unfolded((own_mixed + got[3, 0:HEAD_DIM, :]) * fn_share)
    fn_scaled = fn_grad * fn_scale
    fn_correction = over_points(fn_scaled * fn_summary)
    g_keys = fn_powers[...] * (dot(fn_scaled.astype(BF16), fn_values[...]) - fn_correction)
    g_values = dot(fn_scaled.T.astype(BF16), fn_low[...])
    g_keyval = jnp.concatenate([g_keys, g_values], axis=0).astype(BF16)
    kv_sum = dot_points(fn_hidden[...], g_keyval)
    for half in range(2):
        branch.source[half * D : (half + 1) * D, :] = kv_sum[:, half * D : (half + 1) * D].astype(BF16)
    branch.begin()
    upstream = dot(kv, g_keyval)
    normed, _ = layer_norm(functions_v[...].astype(F32).T)
    own_norm = [to_row(over_points(upstream * normed)), to_row(over_points(upstream))]
    branch_norms = [jnp.where(fn == number, row, 0.0) for number in range(fns) for row in own_norm]
    filled = 8 + len(small) + len(branch_norms)
    last.source[2 * D :, :] = jnp.concatenate(
        [router_sum, *small, *branch_norms, jnp.zeros((32 - filled, D), F32)], axis=0
    ).astype(BF16)
    last.begin()

    waiting = [branch, last, middle, *experts]
    while any(reduction.steps_left for reduction in waiting):
        for reduction in waiting:
            reduction.advance()

    for number, sums in enumerate(experts):
        for half in range(2):
            shared_out[pl.ds(ROW_UP + number * FF + half, D, stride=2), :] = sums.total[
                half * D : (half + 1) * D, :
            ].astype(F32)
        start = ROW_DOWN + number * FF
        shared_out[start : start + FF, :] = sums.total[FF:, :].astype(F32)
    for third in range(3):
        shared_out[pl.ds(ROW_QKV + third, D, stride=3), :] = middle.total[
            third * D : (third + 1) * D, :
        ].astype(F32)
    shared_out[ROW_CROSS_OUT : ROW_CROSS_OUT + D, :] = middle.total[3 * D :, :].astype(F32)
    shared_out[ROW_QUERY : ROW_QUERY + D, :] = last.total[0:D, :].astype(F32)
    shared_out[ROW_SELF_OUT : ROW_SELF_OUT + D, :] = last.total[D : 2 * D, :].astype(F32)
    rest = last.total[2 * D :, :].astype(F32)
    for at, row in enumerate(
        [ROW_GAIN_ONE, ROW_BIAS_ONE, ROW_GAIN_TWO, ROW_BIAS_TWO, ROW_GAIN_THREE, ROW_BIAS_THREE]
    ):
        shared_out[row : row + 1, :] = rest[8 + at : 9 + at]
    router_low = rest[:8].astype(BF16)
    for r in range(EXPERTS):
        spread = dot_points(router_low, pickers[r])
        shared_out[ROW_ROUTER + r : ROW_ROUTER + r + 1, :] = jnp.sum(
            jnp.where(router_mask, spread, 0.0), axis=0, keepdims=True
        )
    for half in range(2):
        branch_rows[pl.ds(2 + half, D, stride=2), :] = branch.total[
            half * D : (half + 1) * D, :
        ].astype(F32)
    own_norm = rest[14:16]
    for number in range(1, fns):
        own_norm = jnp.where(fn == number, rest[14 + 2 * number : 16 + 2 * number], own_norm)
    branch_rows[0:2, :] = own_norm
    for r in range(BRANCH_ROWS):
        branch_out[0:1, r * D : (r + 1) * D] = branch_rows[r : r + 1, :]

    for at in range(4):
        exchange(at).wait_send()
    for reduction in reductions:
        reduction.drain()


def whole_step(fns, pts, points, geometry, functions, presence, fn_counts, item_counts, cotangent, shared, branch):
    rows, fn_rows = points.shape[0], functions.shape[0]
    smem = pl.BlockSpec(memory_space=pltpu.SMEM)
    vmem = pl.BlockSpec(memory_space=pltpu.VMEM)
    anywhere = pl.BlockSpec(memory_space=pl.ANY)
    arrays = (points, geometry, functions, cotangent, shared, branch)

    def low(*shape):
        return pltpu.VMEM(shape, BF16)

    def wide(*shape):
        return pltpu.VMEM(shape, F32)

    scratch = [low(rows, D), low(rows, D), low(fn_rows, D), low(rows, D)]
    scratch += [wide(SHARED_ROWS, D), wide(1, BRANCH_ROWS * D), wide(BRANCH_ROWS, D)]
    scratch += [wide(D, fn_rows), low(D, fn_rows), low(D, fn_rows), low(D, fn_rows), low(FF, rows), low(FF, rows)]
    scratch += [wide(4, HEAD_DIM + 8, D), wide(4, HEAD_DIM + 8, D)]
    scratch += [pltpu.SemaphoreType.DMA((6,)), pltpu.SemaphoreType.DMA((4,)), pltpu.SemaphoreType.DMA((4,))]
    for reduction in plan(fns, pts):
        scratch += reduction.scratch()
    return pl.pallas_call(
        functools.partial(step_kernel, fns, pts),
        out_shape=[low(rows, D), low(rows, D), wide(SHARED_ROWS, D), wide(1, BRANCH_ROWS * D)],
        in_specs=[smem] * 3 + [anywhere] * 6,
        out_specs=[vmem] * 4,
        scratch_shapes=scratch,
        compiler_params=pltpu.CompilerParams(
            collective_id=0, has_side_effects=True, vmem_limit_bytes=36 << 20
        ),
    )(presence, fn_counts, item_counts, *(pltpu.with_memory_space_constraint(value, pltpu.HBM) for value in arrays))


def sgd_update(weights, momentum, average, gradient, step_rate):
    momentum_new = momentum_decay * momentum + gradient
    weights_new = weights - step_rate * (gradient + momentum_decay * momentum_new)
    average_new = average_decay * average + (1.0 - average_decay) * weights_new
    return (weights_new, momentum_new, average_new, weights_new.astype(BF16))


UPDATE_ROWS = 480


def update_kernel(shared_rate, branch_rate, *refs):
    output, input_grad, shared_grad, branch_grad = refs[:4]
    shared_old, branch_old = refs[4:7], refs[7:10]
    output_hbm, input_grad_hbm = refs[10:12]
    shared_new, branch_new, norms_hbm = refs[12:16], refs[16:20], refs[20]
    shared_v, branch_v, norms_v, sems = refs[21:25], refs[25:29], refs[29], refs[30]
    copies = []

    def store(source, target):
        copies.append(pltpu.make_async_copy(source, target, sems.at[len(copies)]))
        copies[-1].start()

    store(output, output_hbm)
    store(input_grad, input_grad_hbm)
    for start in range(0, SHARED_ROWS, UPDATE_ROWS):
        part = slice(start, min(start + UPDATE_ROWS, SHARED_ROWS))
        new = sgd_update(*(ref[part, :] for ref in shared_old), shared_grad[part, :], shared_rate)
        for value, held, target in zip(new, shared_v, shared_new):
            held[part, :] = value
            store(held.at[part, :], target.at[part, :])
    new = sgd_update(*(ref[...] for ref in branch_old), branch_grad[...], branch_rate)
    for value, held, target in zip(new, branch_v, branch_new):
        held[...] = value
        store(held, target)
    norms_v[...] = jnp.concatenate(
        [shared_grad[row : row + 2, :] for row in (ROW_GAIN_ONE, ROW_GAIN_TWO, ROW_GAIN_THREE)], axis=0
    )
    store(norms_v, norms_hbm)
    for copy in copies:
        copy.wait()


def update(shared_rate, branch_rate, output, input_grad, shared_grad, branch_grad, shared_old, branch_old):
    vmem = pl.BlockSpec(memory_space=pltpu.VMEM)
    kinds = [F32, F32, F32, BF16]
    branch_shape = branch_old[0].shape
    outs = [jax.ShapeDtypeStruct(value.shape, BF16) for value in (output, input_grad)]
    outs += [jax.ShapeDtypeStruct((SHARED_ROWS, D), kind) for kind in kinds]
    outs += [jax.ShapeDtypeStruct(branch_shape, kind) for kind in kinds]
    outs += [jax.ShapeDtypeStruct((6, D), F32)]
    parts = -(-SHARED_ROWS // UPDATE_ROWS)
    return pl.pallas_call(
        functools.partial(update_kernel, shared_rate, branch_rate),
        out_shape=outs,
        in_specs=[vmem] * 10,
        out_specs=[pl.BlockSpec(memory_space=pl.ANY)] * len(outs),
        scratch_shapes=[pltpu.VMEM((SHARED_ROWS, D), kind) for kind in kinds]
        + [pltpu.VMEM(branch_shape, kind) for kind in kinds]
        + [pltpu.VMEM((6, D), F32), pltpu.SemaphoreType.DMA((4 * parts + 7,))],
        compiler_params=pltpu.CompilerParams(vmem_limit_bytes=16 << 20),
    )(output, input_grad, shared_grad, branch_grad, *shared_old, *branch_old)


def local(
    fns,
    pts,
    points_in,
    geometry,
    functions,
    presence,
    fn_counts,
    item_counts,
    cotangent,
    shared_weights,
    shared_momentum,
    shared_average,
    branch_weights,
    branch_momentum,
    branch_average,
):
    rows, fn_rows = points_in.shape[1], functions.shape[2]
    shared_old = [value.reshape(SHARED_ROWS, D) for value in (shared_weights, shared_momentum, shared_average)]
    branch_old = [branch_weights, branch_momentum, branch_average]
    step = whole_step(
        fns,
        pts,
        points_in.reshape(rows, D),
        geometry.reshape(rows, D),
        functions.reshape(fn_rows, D),
        presence,
        fn_counts,
        item_counts,
        cotangent.reshape(rows, D),
        shared_old[0],
        branch_weights,
    )
    shared_rate = 0.1 / math.sqrt(pts * rows * fns)
    branch_rate = 0.1 / math.sqrt(pts * fn_rows)
    new = update(shared_rate, branch_rate, *step, shared_old, branch_old)
    return (
        new[0].reshape(1, rows, D),
        new[1].reshape(1, rows, D),
        *(value.reshape(-1) for value in new[2:6]),
        *new[6:10],
        new[10],
    )


def solution(mesh):
    split = P("pts", "fn", None)
    return jax.shard_map(
        functools.partial(local, mesh.shape["fn"], mesh.shape["pts"]),
        mesh=mesh,
        in_specs=(
            split,
            split,
            P("fn", "pts", None, None),
            P("fn", "pts"),
            P("fn", "pts"),
            P("pts"),
            split,
            P(),
            P(),
            P(),
            P("fn", None),
            P("fn", None),
            P("fn", None),
        ),
        out_specs=(
            split,
            split,
            P(),
            P(),
            P(),
            P(),
            P("fn", None),
            P("fn", None),
            P("fn", None),
            P("fn", None),
            P(),
        ),
        check_vma=False,
    )
```

time: 82.8 us -> 65.6 us (0.79)
  other arithmetic: 10 us -> 0 us
  Pallas kernels: 66.8 us -> 60.9 us
  local copies, waits for them, and re-layouts: 2.51 us -> 1.38 us
    pallas_call x1 -> x2, Pallas kernels: 66.8 us -> 60.9 us  [the longest x1 57.9 us: whole_step(): pl.pallas_call(functools.partial(step_kernel, fns, pts), out_shape=[low(r...]
    convert_element_type x2 -> x0, other arithmetic: 5.28 us -> none  [sgd_update(): return (weights_new, momentum_new, average_new, weights_new.astype(BF16))]
    add x2 -> x0, other arithmetic: 2.24 us -> none  [sgd_update(): average_new = average_decay * average + (1.0 - average_decay) * weights_new]
    unnamed x1 -> x0, other arithmetic: 1.88 us -> none
    unnamed x22 -> x12, local copies, waits for them, and re-layouts: 1.82 us -> 1.38 us
where the time goes in v2:
time: 65.6 us; the launch traced here: 65.1 us
  Pallas kernels  60.9 us (93%)
  between operations  2.84 us (4%)
  local copies, waits for them, and re-layouts  1.38 us (2%)
    pallas_call x1, Pallas kernels, whole_step(): pl.pallas_call(functools.partial(step_kernel, fns, pts), out_shape=[low(r...  57.9 us
    pallas_call x1, Pallas kernels, update(): pl.pallas_call(functools.partial(update_kernel, shared_rate, branch_rate)...  3.01 us
    unnamed x12, local copies, waits for them, and re-layouts  1.38 us

profile of v2, /device:TPU:0, one launch (start us, length us, event | category | flops | bytes accessed | tf_op | source)
XLA Modules:
  0.0 65.1 jit_solution(7322592433667524304)
XLA Ops:
  2.6 0.0 copy-start
  2.6 0.0 copy-start.1
  2.6 0.0 copy-start.3
  2.6 0.0 copy-start.4
  2.6 0.0 copy-start.5
  2.6 57.9 %shard_map.212 = (bf16[2048,128]{1,0:T(8,128)(2,1)S(1)}, bf16[2048,128]{1,0:T(8,128)(2,1)S(1)}, f32[2826,128]{1,0:T(8,128)S(1)}, f32[1,33024]{1,0:T(1,128)S(1)}) custom-call(s32[1,1]{1,0:T(1,128)S(6)} %copy.24.refs_0_, s32[1,1]{1,0:T(1,128)S(6)} %copy.25.refs_1_, s32[1]{0:T(128)S(6)} %copy.26.refs_2_, bf16[2048,128]{1,0:T(8,128)(2,1)} %bitcast.17, ...), custom_call_target="tpu_custom_call" | custom-call | tf_op jit(solution)/shard_map/pallas_call | solution.py:685
  60.5 0.0 copy-done
  60.5 0.0 copy-done.1
  60.6 0.0 copy-done.3
  60.6 0.0 copy-done.4
  60.6 0.0 copy-done.5
  60.6 0.0 copy-start.2
  60.6 1.4 %copy-done.2 = f32[361728]{0:T(1024)S(1)} copy-done((f32[361728]{0:T(1024)S(1)}, f32[361728]{0:T(1024)}, u32[]{:S(2)}) %copy-start.2) | copy-done | bytes 1446936
  62.0 3.0 %shard_map.213 = (bf16[2048,128]{1,0:T(8,128)(2,1)}, bf16[2048,128]{1,0:T(8,128)(2,1)}, f32[2826,128]{1,0:T(8,128)}, f32[2826,128]{1,0:T(8,128)}, f32[2826,128]{...) custom-call(bf16[2048,128]{1,0:T(8,128)(2,1)S(1)} %get-tuple-element, ...), custom_call_target="tpu_custom_call" | custom-call | tf_op jit(solution)/shard_map/pallas_call | solution.py:748
Async XLA Ops:
  2.6 58.0 %copy-start = (f32[361728]{0:T(1024)S(1)}, f32[361728]{0:T(1024)}, u32[]{:S(2)}) copy-start(f32[361728]{0:T(1024)} %param.20) | copy-start | bytes 4340740
  2.6 58.0 %copy-start.1 = (f32[361728]{0:T(1024)S(1)}, f32[361728]{0:T(1024)}, u32[]{:S(2)}) copy-start(f32[361728]{0:T(1024)} %param.21) | copy-start | bytes 4340740
  2.6 58.0 %copy-start.3 = (f32[1,33024]{1,0:T(1,128)S(1)}, f32[1,33024]{1,0:T(1,128)}, u32[]{:S(2)}) copy-start(f32[1,33024]{1,0:T(1,128)} %refs_7_.1) | copy-start | bytes 396292
  2.6 58.0 %copy-start.4 = (f32[1,33024]{1,0:T(1,128)S(1)}, f32[1,33024]{1,0:T(1,128)}, u32[]{:S(2)}) copy-start(f32[1,33024]{1,0:T(1,128)} %refs_8_.3) | copy-start | bytes 396292
  2.6 58.0 %copy-start.5 = (f32[1,33024]{1,0:T(1,128)S(1)}, f32[1,33024]{1,0:T(1,128)}, u32[]{:S(2)}) copy-start(f32[1,33024]{1,0:T(1,128)} %refs_9_.1) | copy-start | bytes 396292
  60.6 1.4 %copy-start.2 = (f32[361728]{0:T(1024)S(1)}, f32[361728]{0:T(1024)}, u32[]{:S(2)}) copy-start(f32[361728]{0:T(1024)} %param.22) | copy-start | bytes 4340740

commit v3 on v2

--- a/solution.py
+++ b/solution.py
@@ -44,6 +44,9 @@
 LAST_ROWS = 2 * D + 32
 BRANCH_SENT = 2 * D
 
+EARLY_BACK = 2
+VMEM_LIMIT = 46
+
 
 def dot(a, b):
     return jnp.dot(a, b, preferred_element_type=F32)
@@ -238,17 +241,20 @@
     return 2 if pts % 2 == 0 else 1
 
 
+def middle_size(pts):
+    outer = pts // inner_size(pts)
+    return 2 if outer % 2 == 0 else 1
+
+
 def plan(fns, pts):
-    core = inner_size(pts)
-    outer = pts // core
-    if fns * outer <= 16:
-        everyone, items = [core, fns * outer], [core, outer]
-    else:
-        everyone, items = [core, fns * 4, outer // 4], [core, 4, outer // 4]
-    return [Reduction(everyone, EXPERT_ROWS) for _ in range(EXPERTS)] + [
-        Reduction(everyone, MIDDLE_ROWS),
-        Reduction(everyone, LAST_ROWS),
-        Reduction(items, BRANCH_SENT),
+    core, middle = inner_size(pts), middle_size(pts)
+    far = pts // (core * middle)
+    stepwise = [core, fns * middle, far]
+    at_once = fns * pts <= 32
+    return [Reduction(stepwise, EXPERT_ROWS) for _ in range(EXPERTS)] + [
+        Reduction(stepwise, MIDDLE_ROWS),
+        Reduction([fns * pts] if at_once else stepwise, LAST_ROWS),
+        Reduction([pts] if at_once else [core * middle, far], BRANCH_SENT),
     ]
 
 
@@ -286,7 +292,7 @@
     return jnp.sum(values, axis=1, keepdims=True)
 
 
-def step_kernel(fns, pts, *refs):
+def step_kernel(fns, pts, shared_rate, branch_rate, *refs):
     refs = list(refs)
 
     def take(n):
@@ -296,9 +302,12 @@
 
     presence, fn_counts, item_counts = take(3)
     points_hbm, geometry_hbm, functions_hbm, cotangent_hbm, shared_hbm, branch_hbm = take(6)
-    output, input_grad, shared_out, branch_out = take(4)
-    points_v, geometry_v, functions_v, cotangent_v, shared_v, branch_v, branch_rows = take(7)
-    fn_powers, fn_low, fn_values, fn_hidden, hidden_v, pre_v = take(6)
+    momenta_hbm = take(4)
+    output, input_grad = take(2)
+    shared_new, branch_new, norms_out = take(4), take(4), take(1)[0]
+    shared_v, branch_v = shared_new[0], branch_new[0]
+    points_v, geometry_v, functions_v, cotangent_v, branch_rows, shared_sum, branch_sum = take(7)
+    fn_powers, fn_low, fn_values, fn_hidden, hidden_v, pre_v, back_v, up_t, down_t = take(9)
     sent, got = take(2)
     local_sem, x_send, x_recv = take(3)
     reductions = plan(fns, pts)
@@ -306,33 +315,37 @@
     assert not refs
 
     fn, pt = lax.axis_index("fn"), lax.axis_index("pts")
-    core_size = inner_size(pts)
-    outer_size = pts // core_size
-    outer, core = pt // core_size, pt % core_size
-    core_level = Level(core_size, core, lambda j: (fn, outer * core_size + j))
-    if fns * outer_size <= 16:
-        everyone = [
-            core_level,
-            Level(
-                fns * outer_size,
-                fn * outer_size + outer,
-                lambda j: (j // outer_size, j % outer_size * core_size + core),
-            ),
-        ]
-        items = [core_level, Level(outer_size, outer, lambda j: (fn, j * core_size + core))]
+    core_size, middle_size_ = inner_size(pts), middle_size(pts)
+    near_size = core_size * middle_size_
+    far, near = pt // near_size, pt % near_size
+    middle_at, core = near // core_size, near % core_size
+    far_level = Level(pts // near_size, far, lambda j: (fn, j * near_size + near))
+    stepwise = [
+        Level(core_size, core, lambda j: (fn, pt - core + j)),
+        Level(
+            fns * middle_size_,
+            fn * middle_size_ + middle_at,
+            lambda j: (j // middle_size_, far * near_size + j % middle_size_ * core_size + core),
+        ),
+        far_level,
+    ]
+    if fns * pts <= 32:
+        everyone = [Level(fns * pts, fn * pts + pt, lambda j: (j // pts, j % pts))]
+        items = [Level(pts, pt, lambda j: (fn, j))]
         greeted = everyone
     else:
-        far, near = outer // 4, outer % 4
-        far_level = Level(outer_size // 4, far, lambda j: (fn, (j * 4 + near) * core_size + core))
-        everyone = [
-            core_level,
-            Level(fns * 4, fn * 4 + near, lambda j: (j // 4, (far * 4 + j % 4) * core_size + core)),
+        everyone = stepwise
+        items = [Level(near_size, near, lambda j: (fn, far * near_size + j)), far_level]
+        greeted = [
+            Level(
+                fns * near_size,
+                fn * near_size + near,
+                lambda j: (j // near_size, far * near_size + j % near_size),
+            ),
             far_level,
         ]
-        items = [core_level, Level(4, near, lambda j: (fn, (far * 4 + j) * core_size + core)), far_level]
-        greeted = everyone
-    for reduction, scratch in zip(reductions, bound):
-        reduction.bind(scratch, items if reduction is reductions[-1] else everyone)
+    for at, (reduction, scratch) in enumerate(zip(reductions, bound)):
+        reduction.bind(scratch, stepwise if at <= EXPERTS else everyone if at == EXPERTS + 1 else items)
     experts, middle, last, branch = reductions[:EXPERTS], *reductions[EXPERTS:]
 
     rows, fn_rows = points_v.shape[0], functions_v.shape[0]
@@ -346,6 +359,7 @@
             (points_hbm, points_v),
             (geometry_hbm, geometry_v),
             (cotangent_hbm, cotangent_v),
+            *zip(momenta_hbm, [*shared_new[1:3], *branch_new[1:3]]),
         ]
     ):
         loads.append(pltpu.make_async_copy(source, target, local_sem.at[at]))
@@ -439,6 +453,11 @@
     self_w = shared_rows(ROW_SELF_OUT)
     qkv_w = jnp.concatenate([shared_rows(ROW_QKV + third, 3) for third in range(3)], axis=1)
 
+    for piece_at in range(2 * EXPERTS):
+        number, half = piece_at // 2, piece_at % 2
+        up_t[piece_at * D : (piece_at + 1) * D, :] = shared_rows(ROW_UP + number * FF + half, 2).T
+        down_t[:, piece_at * D : (piece_at + 1) * D] = shared_rows(ROW_DOWN + piece_at * D).T
+
     expert_at = lax.broadcasted_iota(jnp.int32, (8, D), 0)
     router_mask = lax.broadcasted_iota(jnp.int32, (8, D), 1) % EXPERTS == expert_at
     router_t = jnp.zeros((8, D), F32)
@@ -498,6 +517,9 @@
     loads[5].wait()
     arriving = cotangent_v[...].astype(F32).T
     arriving_low = arriving.astype(BF16)
+    for number in range(EARLY_BACK):
+        down = shared_v[ROW_DOWN + number * FF : ROW_DOWN + (number + 1) * FF, :].astype(BF16)
+        back_v[number * FF : (number + 1) * FF, :] = dot(down, arriving_low)
 
     exchange(1).wait_recv()
     other_max = to_column(got[1, HEAD_DIM : HEAD_DIM + 1, :])
@@ -514,52 +536,61 @@
     normed_three, inverse_three = layer_norm(after_self)
     hidden_three = (normed_three * gain_three + bias_three).astype(BF16)
 
-    result, upstream, gate_grads = after_self, None, []
+    def expert_sums(number):
+        part = slice(number * FF, (number + 1) * FF)
+        source = experts[number].source
+        up_sum = dot_points(hidden_three, pre_v[part, :])
+        source[0:D, :] = up_sum[:, :D].astype(BF16)
+        source[D : 2 * D, :] = up_sum[:, D:].astype(BF16)
+        source[FF:, :] = dot_points(hidden_v[part, :], arriving_low).astype(BF16)
+        experts[number].begin()
+
+    def advance(*numbers):
+        for number in numbers:
+            reductions[number].advance()
+
+    upstream, gate_grads = None, []
     for number in range(EXPERTS):
-        up = jnp.concatenate([shared_rows(ROW_UP + number * FF + half, 2) for half in range(2)], axis=1)
-        down = jnp.concatenate(
-            [shared_rows(ROW_DOWN + number * FF + half * D) for half in range(2)], axis=0
-        )
+        part = slice(number * FF, (number + 1) * FF)
         gate = half_gates[number : number + 1]
-        argument = dot(up.T, hidden_three)
-        back = dot(down, arriving_low)
+        argument = dot(up_t[part, :], hidden_three)
+        if number < EARLY_BACK:
+            back = back_v[part, :]
+        else:
+            back = dot(shared_v[ROW_DOWN + number * FF : ROW_DOWN + (number + 1) * FF, :].astype(BF16), arriving_low)
         scaled = argument * math.sqrt(0.5)
         twice_cdf = 1.0 + lax.erf(scaled)
         bell = jnp.exp2(scaled * scaled * -math.log2(math.e)) * (2.0 / math.sqrt(math.pi))
         active = argument * twice_cdf
         gate_grads.append(0.5 * jnp.sum(active * back, axis=0, keepdims=True))
-        hidden_v[...] = (active * gate).astype(BF16)
-        pre_v[...] = (back * gate * (twice_cdf + scaled * bell)).astype(BF16)
-        result = result + dot(down.T, hidden_v[...])
-        part = dot(up, pre_v[...])
-        upstream = part if upstream is None else upstream + part
-        sums = experts[number]
-        up_sum = dot_points(hidden_three, pre_v[...])
-        sums.source[0:D, :] = up_sum[:, :D].astype(BF16)
-        sums.source[D : 2 * D, :] = up_sum[:, D:].astype(BF16)
-        sums.source[FF:, :] = dot_points(hidden_v[...], arriving_low).astype(BF16)
-        sums.begin()
-        for earlier in experts[:number]:
-            earlier.advance()
-    output[...] = result.T.astype(BF16)
+        hidden_v[part, :] = (active * gate).astype(BF16)
+        pre_v[part, :] = (back * gate * (twice_cdf + scaled * bell)).astype(BF16)
+        up = jnp.concatenate([shared_rows(ROW_UP + number * FF + half, 2) for half in range(2)], axis=1)
+        more = dot(up, pre_v[part, :])
+        upstream = more if upstream is None else upstream + more
+        if number + 1 < EXPERTS:
+            expert_sums(number)
+            if number:
+                advance(number - 1)
 
     gate_grads = jnp.concatenate(gate_grads, axis=0)
     g_logits = gates * (gate_grads - jnp.sum(gates * gate_grads, axis=0, keepdims=True))
     g_logits = jnp.concatenate([g_logits, jnp.zeros_like(g_logits)], axis=0).astype(BF16)
-    router_sum = dot(g_logits, geometry_v[...])
-    small = [None] * 6
-    small[4] = to_row(over_points(upstream * normed_three))
-    small[5] = to_row(over_points(upstream))
     g_after_self = arriving + norm_back(normed_three, inverse_three, gain_three, upstream)
     g_proj = g_after_self.astype(BF16)
     g_self_out = dot(self_w, g_proj).astype(BF16)
     own_grad = folded(dot_points(self_weights, g_self_out))
     sent[2, 0:HEAD_DIM, :] = own_grad
     exchange(2).start()
-    for earlier in experts:
-        earlier.advance()
+    expert_sums(EXPERTS - 1)
+    advance(2, 0)
+    router_sum = dot(g_logits, geometry_v[...])
+    small = [None] * 6
+    small[4] = to_row(over_points(upstream * normed_three))
+    small[5] = to_row(over_points(upstream))
     last.source[D : 2 * D, :] = dot_points(self_out, g_proj).astype(BF16)
     g_queries = feature_softmax_back(self_soft, dot(self_low, g_self_out)).astype(BF16)
+    advance(3, 1)
 
     exchange(2).wait_recv()
     scaled_grad = unfolded(own_grad + got[2, 0:HEAD_DIM, :]) * own_factor
@@ -568,31 +599,28 @@
     g_values = dot(scaled_grad.T.astype(BF16), key_low)
     g_qkv = jnp.concatenate([g_queries, g_keys.astype(BF16), g_values.astype(BF16)], axis=0)
     upstream = dot(qkv_w, g_qkv)
-    small[2] = to_row(over_points(upstream * normed_two))
-    small[3] = to_row(over_points(upstream))
     g_after_cross = g_after_self + norm_back(normed_two, inverse_two, gain_two, upstream)
     g_proj = g_after_cross.astype(BF16)
     g_cross_out = dot(cross_w, g_proj).astype(BF16)
     own_mixed = folded(dot_points(cross_low, g_cross_out))
     sent[3, 0:HEAD_DIM, :] = own_mixed
     exchange(3).start()
+    advance(0, 2)
     qkv_sum = dot_points(hidden_two, g_qkv)
     for third in range(3):
         middle.source[third * D : (third + 1) * D, :] = qkv_sum[:, third * D : (third + 1) * D].astype(BF16)
     middle.source[3 * D :, :] = dot_points(cross_out, g_proj).astype(BF16)
     middle.begin()
-    for earlier in experts:
-        earlier.advance()
+    small[2] = to_row(over_points(upstream * normed_two))
+    small[3] = to_row(over_points(upstream))
 
     g_query = feature_softmax_back(cross_soft, dot(mixed_low, g_cross_out)).astype(BF16)
-    upstream = dot(query_w, g_query)
-    small[0] = to_row(over_points(upstream * normed_one))
-    small[1] = to_row(over_points(upstream))
-    total = g_after_cross + norm_back(normed_one, inverse_one, gain_one, upstream)
-    input_grad[...] = total.T.astype(BF16)
+    advance(1, 3)
+    upstream_one = dot(query_w, g_query)
     last.source[0:D, :] = dot_points(hidden_one, g_query).astype(BF16)
-    for earlier in [middle, *experts]:
-        earlier.advance()
+    small[0] = to_row(over_points(upstream_one * normed_one))
+    small[1] = to_row(over_points(upstream_one))
+    advance(4)
 
     exchange(3).wait_recv()
     fn_grad = unfolded((own_mixed + got[3, 0:HEAD_DIM, :]) * fn_share)
@@ -615,83 +643,83 @@
     ).astype(BF16)
     last.begin()
 
-    waiting = [branch, last, middle, *experts]
-    while any(reduction.steps_left for reduction in waiting):
-        for reduction in waiting:
-            reduction.advance()
+    total = g_after_cross + norm_back(normed_one, inverse_one, gain_one, upstream_one)
+    input_grad[...] = total.T.astype(BF16)
+    advance(0, 2, 1, 3)
+    branch.advance()
+    last.advance()
+    result = after_self + dot(down_t[...], hidden_v[...])
+    output[...] = result.T.astype(BF16)
+    advance(4, 0, 1, 2, 3, 4, 0, 1, 2, 3, 4, 0, 1)
+
+    for load in loads[6:]:
+        load.wait()
+    waiting = [*experts, middle, branch, last]
+
+    def finish(reduction):
+        while reduction.steps_left:
+            for other in waiting:
+                if other is reduction or len(other.steps_left) > 1:
+                    other.advance()
+
+    def renew(start, count):
+        part = slice(start, start + count)
+        new = sgd_update(*(ref[part, :] for ref in shared_new[:3]), shared_sum[part, :], shared_rate)
+        for value, target in zip(new, shared_new):
+            target[part, :] = value
 
     for number, sums in enumerate(experts):
+        finish(sums)
         for half in range(2):
-            shared_out[pl.ds(ROW_UP + number * FF + half, D, stride=2), :] = sums.total[
+            shared_sum[pl.ds(ROW_UP + number * FF + half, D, stride=2), :] = sums.total[
                 half * D : (half + 1) * D, :
             ].astype(F32)
         start = ROW_DOWN + number * FF
-        shared_out[start : start + FF, :] = sums.total[FF:, :].astype(F32)
+        shared_sum[start : start + FF, :] = sums.total[FF:, :].astype(F32)
+    whole = -(-ROW_UP // 16) * 16
+    renew(whole, SHARED_ROWS - whole)
+    finish(middle)
     for third in range(3):
-        shared_out[pl.ds(ROW_QKV + third, D, stride=3), :] = middle.total[
+        shared_sum[pl.ds(ROW_QKV + third, D, stride=3), :] = middle.total[
             third * D : (third + 1) * D, :
         ].astype(F32)
-    shared_out[ROW_CROSS_OUT : ROW_CROSS_OUT + D, :] = middle.total[3 * D :, :].astype(F32)
-    shared_out[ROW_QUERY : ROW_QUERY + D, :] = last.total[0:D, :].astype(F32)
-    shared_out[ROW_SELF_OUT : ROW_SELF_OUT + D, :] = last.total[D : 2 * D, :].astype(F32)
+    shared_sum[ROW_CROSS_OUT : ROW_CROSS_OUT + D, :] = middle.total[3 * D :, :].astype(F32)
+    finish(branch)
+    for half in range(2):
+        branch_rows[pl.ds(2 + half, D, stride=2), :] = branch.total[
+            half * D : (half + 1) * D, :
+        ].astype(F32)
+    for r in range(2, BRANCH_ROWS):
+        branch_sum[0:1, r * D : (r + 1) * D] = branch_rows[r : r + 1, :]
+    finish(last)
+    shared_sum[ROW_QUERY : ROW_QUERY + D, :] = last.total[0:D, :].astype(F32)
+    shared_sum[ROW_SELF_OUT : ROW_SELF_OUT + D, :] = last.total[D : 2 * D, :].astype(F32)
     rest = last.total[2 * D :, :].astype(F32)
     for at, row in enumerate(
         [ROW_GAIN_ONE, ROW_BIAS_ONE, ROW_GAIN_TWO, ROW_BIAS_TWO, ROW_GAIN_THREE, ROW_BIAS_THREE]
     ):
-        shared_out[row : row + 1, :] = rest[8 + at : 9 + at]
+        shared_sum[row : row + 1, :] = rest[8 + at : 9 + at]
+    norms_out[...] = rest[8:14]
     router_low = rest[:8].astype(BF16)
     for r in range(EXPERTS):
         spread = dot_points(router_low, pickers[r])
-        shared_out[ROW_ROUTER + r : ROW_ROUTER + r + 1, :] = jnp.sum(
+        shared_sum[ROW_ROUTER + r : ROW_ROUTER + r + 1, :] = jnp.sum(
             jnp.where(router_mask, spread, 0.0), axis=0, keepdims=True
         )
-    for half in range(2):
-        branch_rows[pl.ds(2 + half, D, stride=2), :] = branch.total[
-            half * D : (half + 1) * D, :
-        ].astype(F32)
+    renew(0, whole)
     own_norm = rest[14:16]
     for number in range(1, fns):
         own_norm = jnp.where(fn == number, rest[14 + 2 * number : 16 + 2 * number], own_norm)
-    branch_rows[0:2, :] = own_norm
-    for r in range(BRANCH_ROWS):
-        branch_out[0:1, r * D : (r + 1) * D] = branch_rows[r : r + 1, :]
+    for r in range(2):
+        branch_sum[0:1, r * D : (r + 1) * D] = own_norm[r : r + 1]
+    new = sgd_update(*(ref[...] for ref in branch_new[:3]), branch_sum[...], branch_rate)
+    for value, target in zip(new, branch_new):
+        target[...] = value
 
     for at in range(4):
         exchange(at).wait_send()
     for reduction in reductions:
         reduction.drain()
-
-
-def whole_step(fns, pts, points, geometry, functions, presence, fn_counts, item_counts, cotangent, shared, branch):
-    rows, fn_rows = points.shape[0], functions.shape[0]
-    smem = pl.BlockSpec(memory_space=pltpu.SMEM)
-    vmem = pl.BlockSpec(memory_space=pltpu.VMEM)
-    anywhere = pl.BlockSpec(memory_space=pl.ANY)
-    arrays = (points, geometry, functions, cotangent, shared, branch)
-
-    def low(*shape):
-        return pltpu.VMEM(shape, BF16)
-
-    def wide(*shape):
-        return pltpu.VMEM(shape, F32)
-
-    scratch = [low(rows, D), low(rows, D), low(fn_rows, D), low(rows, D)]
-    scratch += [wide(SHARED_ROWS, D), wide(1, BRANCH_ROWS * D), wide(BRANCH_ROWS, D)]
-    scratch += [wide(D, fn_rows), low(D, fn_rows), low(D, fn_rows), low(D, fn_rows), low(FF, rows), low(FF, rows)]
-    scratch += [wide(4, HEAD_DIM + 8, D), wide(4, HEAD_DIM + 8, D)]
-    scratch += [pltpu.SemaphoreType.DMA((6,)), pltpu.SemaphoreType.DMA((4,)), pltpu.SemaphoreType.DMA((4,))]
-    for reduction in plan(fns, pts):
-        scratch += reduction.scratch()
-    return pl.pallas_call(
-        functools.partial(step_kernel, fns, pts),
-        out_shape=[low(rows, D), low(rows, D), wide(SHARED_ROWS, D), wide(1, BRANCH_ROWS * D)],
-        in_specs=[smem] * 3 + [anywhere] * 6,
-        out_specs=[vmem] * 4,
-        scratch_shapes=scratch,
-        compiler_params=pltpu.CompilerParams(
-            collective_id=0, has_side_effects=True, vmem_limit_bytes=36 << 20
-        ),
-    )(presence, fn_counts, item_counts, *(pltpu.with_memory_space_constraint(value, pltpu.HBM) for value in arrays))
 
 
 def sgd_update(weights, momentum, average, gradient, step_rate):
@@ -701,60 +729,65 @@
     return (weights_new, momentum_new, average_new, weights_new.astype(BF16))
 
 
-UPDATE_ROWS = 480
-
-
-def update_kernel(shared_rate, branch_rate, *refs):
-    output, input_grad, shared_grad, branch_grad = refs[:4]
-    shared_old, branch_old = refs[4:7], refs[7:10]
-    output_hbm, input_grad_hbm = refs[10:12]
-    shared_new, branch_new, norms_hbm = refs[12:16], refs[16:20], refs[20]
-    shared_v, branch_v, norms_v, sems = refs[21:25], refs[25:29], refs[29], refs[30]
-    copies = []
-
-    def store(source, target):
-        copies.append(pltpu.make_async_copy(source, target, sems.at[len(copies)]))
-        copies[-1].start()
-
-    store(output, output_hbm)
-    store(input_grad, input_grad_hbm)
-    for start in range(0, SHARED_ROWS, UPDATE_ROWS):
-        part = slice(start, min(start + UPDATE_ROWS, SHARED_ROWS))
-        new = sgd_update(*(ref[part, :] for ref in shared_old), shared_grad[part, :], shared_rate)
-        for value, held, target in zip(new, shared_v, shared_new):
-            held[part, :] = value
-            store(held.at[part, :], target.at[part, :])
-    new = sgd_update(*(ref[...] for ref in branch_old), branch_grad[...], branch_rate)
-    for value, held, target in zip(new, branch_v, branch_new):
-        held[...] = value
-        store(held, target)
-    norms_v[...] = jnp.concatenate(
-        [shared_grad[row : row + 2, :] for row in (ROW_GAIN_ONE, ROW_GAIN_TWO, ROW_GAIN_THREE)], axis=0
-    )
-    store(norms_v, norms_hbm)
+def low(*shape):
+    return pltpu.VMEM(shape, BF16)
+
+
+def wide(*shape):
+    return pltpu.VMEM(shape, F32)
+
+
+def whole_step(fns, pts, rates, counts, arrays, momenta):
+    points, _, functions = arrays[:3]
+    rows, fn_rows = points.shape[0], functions.shape[0]
+    smem = pl.BlockSpec(memory_space=pltpu.SMEM)
+    vmem = pl.BlockSpec(memory_space=pltpu.VMEM)
+    anywhere = pl.BlockSpec(memory_space=pl.ANY)
+    branch = (1, BRANCH_ROWS * D)
+
+    outs = [low(rows, D), low(rows, D)]
+    outs += [wide(SHARED_ROWS, D)] * 3 + [low(SHARED_ROWS, D)] + [wide(*branch)] * 3 + [low(*branch)] + [wide(6, D)]
+    scratch = [low(rows, D), low(rows, D), low(fn_rows, D), low(rows, D)]
+    scratch += [wide(BRANCH_ROWS, D), wide(SHARED_ROWS, D), wide(*branch)]
+    scratch += [wide(D, fn_rows), low(D, fn_rows), low(D, fn_rows), low(D, fn_rows), low(HIDDEN, rows), low(HIDDEN, rows)]
+    scratch += [wide(max(EARLY_BACK, 1) * FF, rows), low(HIDDEN, D), low(D, HIDDEN)]
+    scratch += [wide(4, HEAD_DIM + 8, D), wide(4, HEAD_DIM + 8, D)]
+    scratch += [pltpu.SemaphoreType.DMA((10,)), pltpu.SemaphoreType.DMA((4,)), pltpu.SemaphoreType.DMA((4,))]
+    for reduction in plan(fns, pts):
+        scratch += reduction.scratch()
+    return pl.pallas_call(
+        functools.partial(step_kernel, fns, pts, *rates),
+        out_shape=outs,
+        in_specs=[smem] * 3 + [anywhere] * (len(arrays) + len(momenta)),
+        out_specs=[vmem] * len(outs),
+        scratch_shapes=scratch,
+        compiler_params=pltpu.CompilerParams(
+            collective_id=0, has_side_effects=True, vmem_limit_bytes=VMEM_LIMIT << 20
+        ),
+    )(*counts, *(pltpu.with_memory_space_constraint(value, pltpu.HBM) for value in (*arrays, *momenta)))
+
+
+def store_kernel(count, *refs):
+    copies = [
+        pltpu.make_async_copy(source, target, refs[-1].at[at])
+        for at, (source, target) in enumerate(zip(refs[:count], refs[count:]))
+    ]
+    for copy in copies:
+        copy.start()
     for copy in copies:
         copy.wait()
 
 
-def update(shared_rate, branch_rate, output, input_grad, shared_grad, branch_grad, shared_old, branch_old):
-    vmem = pl.BlockSpec(memory_space=pltpu.VMEM)
-    kinds = [F32, F32, F32, BF16]
-    branch_shape = branch_old[0].shape
-    outs = [jax.ShapeDtypeStruct(value.shape, BF16) for value in (output, input_grad)]
-    outs += [jax.ShapeDtypeStruct((SHARED_ROWS, D), kind) for kind in kinds]
-    outs += [jax.ShapeDtypeStruct(branch_shape, kind) for kind in kinds]
-    outs += [jax.ShapeDtypeStruct((6, D), F32)]
-    parts = -(-SHARED_ROWS // UPDATE_ROWS)
+def stored(values):
+    count = len(values)
     return pl.pallas_call(
-        functools.partial(update_kernel, shared_rate, branch_rate),
-        out_shape=outs,
-        in_specs=[vmem] * 10,
-        out_specs=[pl.BlockSpec(memory_space=pl.ANY)] * len(outs),
-        scratch_shapes=[pltpu.VMEM((SHARED_ROWS, D), kind) for kind in kinds]
-        + [pltpu.VMEM(branch_shape, kind) for kind in kinds]
-        + [pltpu.VMEM((6, D), F32), pltpu.SemaphoreType.DMA((4 * parts + 7,))],
-        compiler_params=pltpu.CompilerParams(vmem_limit_bytes=16 << 20),
-    )(output, input_grad, shared_grad, branch_grad, *shared_old, *branch_old)
+        functools.partial(store_kernel, count),
+        out_shape=[jax.ShapeDtypeStruct(value.shape, value.dtype) for value in values],
+        in_specs=[pl.BlockSpec(memory_space=pltpu.VMEM)] * count,
+        out_specs=[pl.BlockSpec(memory_space=pl.ANY)] * count,
+        scratch_shapes=[pltpu.SemaphoreType.DMA((count,))],
+        compiler_params=pltpu.CompilerParams(vmem_limit_bytes=4 << 20),
+    )(*values)
 
 
 def local(
@@ -775,30 +808,23 @@
     branch_average,
 ):
     rows, fn_rows = points_in.shape[1], functions.shape[2]
-    shared_old = [value.reshape(SHARED_ROWS, D) for value in (shared_weights, shared_momentum, shared_average)]
-    branch_old = [branch_weights, branch_momentum, branch_average]
-    step = whole_step(
-        fns,
-        pts,
+    rates = (0.1 / math.sqrt(pts * rows * fns), 0.1 / math.sqrt(pts * fn_rows))
+    arrays = [
         points_in.reshape(rows, D),
         geometry.reshape(rows, D),
         functions.reshape(fn_rows, D),
-        presence,
-        fn_counts,
-        item_counts,
         cotangent.reshape(rows, D),
-        shared_old[0],
+        shared_weights.reshape(SHARED_ROWS, D),
         branch_weights,
-    )
-    shared_rate = 0.1 / math.sqrt(pts * rows * fns)
-    branch_rate = 0.1 / math.sqrt(pts * fn_rows)
-    new = update(shared_rate, branch_rate, *step, shared_old, branch_old)
+    ]
+    momenta = [value.reshape(SHARED_ROWS, D) for value in (shared_momentum, shared_average)]
+    momenta += [branch_momentum, branch_average]
+    new = stored(whole_step(fns, pts, rates, (presence, fn_counts, item_counts), arrays, momenta))
     return (
         new[0].reshape(1, rows, D),
         new[1].reshape(1, rows, D),
         *(value.reshape(-1) for value in new[2:6]),
-        *new[6:10],
-        new[10],
+        *new[6:],
     )
 
 

time: 65.6 us -> 57.9 us (0.88)
  Pallas kernels: 60.9 us -> 55 us
  local copies, waits for them, and re-layouts: 1.38 us -> 0 us
    pallas_call x2, Pallas kernels: 60.9 us -> 55 us  [the longest x1 52.1 us: whole_step(): pl.pallas_call(functools.partial(step_kernel, fns, pts, *rates), out_shap...]
    unnamed x12 -> x0, local copies, waits for them, and re-layouts: 1.38 us -> none
where the time goes in v3:
time: 57.9 us; the launch traced here: 57.7 us
  Pallas kernels  55 us (95%)
  between operations  2.75 us (5%)
    pallas_call x1, Pallas kernels, whole_step(): pl.pallas_call(functools.partial(step_kernel, fns, pts, *rates), out_shap...  52.1 us
    pallas_call x1, Pallas kernels, stored(): pl.pallas_call(functools.partial(store_kernel, count), out_shape=[jax.Sha...  2.88 us

profile of v3, /device:TPU:0, one launch (start us, length us, event | category | flops | bytes accessed | tf_op | source)
XLA Modules:
  0.0 57.7 jit_solution(15446121110549143165)
XLA Ops:
  2.6 52.1 %shard_map.212 = (bf16[2048,128]{1,0:T(8,128)(2,1)S(1)}, bf16[2048,128]{1,0:T(8,128)(2,1)S(1)}, f32[2826,128]{1,0:T(8,128)S(1)}, f32[2826,128]{1,0:T(8,128)S(1)}...) custom-call(s32[1,1]{1,0:T(1,128)S(6)} %copy.24.refs_0_, ...), custom_call_target="tpu_custom_call" | custom-call | tf_op jit(solution)/shard_map/pallas_call | solution.py:758
  54.7 2.9 %shard_map.213 = (bf16[2048,128]{1,0:T(8,128)(2,1)}, bf16[2048,128]{1,0:T(8,128)(2,1)}, f32[2826,128]{1,0:T(8,128)}, f32[2826,128]{1,0:T(8,128)}, f32[2826,128]{...) custom-call(bf16[2048,128]{1,0:T(8,128)(2,1)S(1)} %get-tuple-element, ...), custom_call_target="tpu_custom_call" | custom-call | tf_op jit(solution)/shard_map/pallas_call | solution.py:783

commit v4 on v3

--- a/solution.py
+++ b/solution.py
@@ -40,12 +40,12 @@
 BRANCH_ROWS = 2 + 2 * D
 
 EXPERT_ROWS = 2 * FF
-MIDDLE_ROWS = 4 * D
+EARLY_ROWS = 2 * D
+MIDDLE_ROWS = 2 * D
 LAST_ROWS = 2 * D + 32
-BRANCH_SENT = 2 * D
-
-EARLY_BACK = 2
-VMEM_LIMIT = 46
+BRANCH_SENT = 2 * D + 32
+
+VMEM_LIMIT = 52
 
 
 def dot(a, b):
@@ -250,11 +250,19 @@
     core, middle = inner_size(pts), middle_size(pts)
     far = pts // (core * middle)
     stepwise = [core, fns * middle, far]
-    at_once = fns * pts <= 32
-    return [Reduction(stepwise, EXPERT_ROWS) for _ in range(EXPERTS)] + [
-        Reduction(stepwise, MIDDLE_ROWS),
-        Reduction([fns * pts] if at_once else stepwise, LAST_ROWS),
-        Reduction([pts] if at_once else [core * middle, far], BRANCH_SENT),
+    small = fns * pts <= 32
+    halved = [core, fns * middle * far] if small else stepwise
+    at_once = [fns * pts] if small else stepwise
+    items = [pts] if small else [core * middle, far]
+    return [
+        Reduction(stepwise, EXPERT_ROWS),
+        Reduction(stepwise, EXPERT_ROWS),
+        Reduction(halved, EXPERT_ROWS),
+        Reduction(halved, EXPERT_ROWS),
+        Reduction(halved, EARLY_ROWS),
+        Reduction(halved, MIDDLE_ROWS),
+        Reduction(at_once, LAST_ROWS),
+        Reduction(items, BRANCH_SENT),
     ]
 
 
@@ -307,7 +315,7 @@
     shared_new, branch_new, norms_out = take(4), take(4), take(1)[0]
     shared_v, branch_v = shared_new[0], branch_new[0]
     points_v, geometry_v, functions_v, cotangent_v, branch_rows, shared_sum, branch_sum = take(7)
-    fn_powers, fn_low, fn_values, fn_hidden, hidden_v, pre_v, back_v, up_t, down_t = take(9)
+    fn_powers, fn_low, fn_values, fn_normed, hidden_v, pre_v, back_v, g_expert_v, up_t, down_t = take(10)
     sent, got = take(2)
     local_sem, x_send, x_recv = take(3)
     reductions = plan(fns, pts)
@@ -330,11 +338,20 @@
         far_level,
     ]
     if fns * pts <= 32:
-        everyone = [Level(fns * pts, fn * pts + pt, lambda j: (j // pts, j % pts))]
+        outer = pts // core_size
+        halved = [
+            stepwise[0],
+            Level(
+                fns * outer,
+                fn * outer + pt // core_size,
+                lambda j: (j // outer, j % outer * core_size + core),
+            ),
+        ]
+        at_once = [Level(fns * pts, fn * pts + pt, lambda j: (j // pts, j % pts))]
         items = [Level(pts, pt, lambda j: (fn, j))]
-        greeted = everyone
+        greeted = at_once
     else:
-        everyone = stepwise
+        halved = at_once = stepwise
         items = [Level(near_size, near, lambda j: (fn, far * near_size + j)), far_level]
         greeted = [
             Level(
@@ -344,9 +361,11 @@
             ),
             far_level,
         ]
-    for at, (reduction, scratch) in enumerate(zip(reductions, bound)):
-        reduction.bind(scratch, stepwise if at <= EXPERTS else everyone if at == EXPERTS + 1 else items)
-    experts, middle, last, branch = reductions[:EXPERTS], *reductions[EXPERTS:]
+    ways = [stepwise, stepwise, halved, halved, halved, halved, at_once, items]
+    for reduction, scratch, levels in zip(reductions, bound, ways):
+        reduction.bind(scratch, levels)
+    experts = reductions[:EXPERTS]
+    early, middle, last, branch = reductions[EXPERTS:]
 
     rows, fn_rows = points_v.shape[0], functions_v.shape[0]
 
@@ -427,7 +446,7 @@
     loads[1].wait()
     normed, _ = layer_norm(functions_v[...].astype(F32).T)
     hidden = (normed * branch_gain + branch_bias).astype(BF16)
-    fn_hidden[...] = hidden
+    fn_normed[...] = normed.astype(BF16)
     keyval = dot(kv.T, hidden)
     keys = jnp.where(fn_usable, keyval[:D], far_below)
     fn_values[...] = keyval[D:].astype(BF16)
@@ -516,10 +535,11 @@
     half_gates = 0.5 * gates
     loads[5].wait()
     arriving = cotangent_v[...].astype(F32).T
-    arriving_low = arriving.astype(BF16)
-    for number in range(EARLY_BACK):
+    for number in range(EXPERTS):
+        g_expert = (half_gates[number : number + 1] * arriving).astype(BF16)
+        g_expert_v[number * D : (number + 1) * D, :] = g_expert
         down = shared_v[ROW_DOWN + number * FF : ROW_DOWN + (number + 1) * FF, :].astype(BF16)
-        back_v[number * FF : (number + 1) * FF, :] = dot(down, arriving_low)
+        back_v[number * FF : (number + 1) * FF, :] = dot(down, g_expert)
 
     exchange(1).wait_recv()
     other_max = to_column(got[1, HEAD_DIM : HEAD_DIM + 1, :])
@@ -542,39 +562,36 @@
         up_sum = dot_points(hidden_three, pre_v[part, :])
         source[0:D, :] = up_sum[:, :D].astype(BF16)
         source[D : 2 * D, :] = up_sum[:, D:].astype(BF16)
-        source[FF:, :] = dot_points(hidden_v[part, :], arriving_low).astype(BF16)
+        source[FF:, :] = dot_points(hidden_v[part, :], g_expert_v[number * D : (number + 1) * D, :]).astype(BF16)
         experts[number].begin()
 
     def advance(*numbers):
         for number in numbers:
             reductions[number].advance()
 
-    upstream, gate_grads = None, []
+    upstream, gated_grads = None, []
     for number in range(EXPERTS):
         part = slice(number * FF, (number + 1) * FF)
-        gate = half_gates[number : number + 1]
         argument = dot(up_t[part, :], hidden_three)
-        if number < EARLY_BACK:
-            back = back_v[part, :]
-        else:
-            back = dot(shared_v[ROW_DOWN + number * FF : ROW_DOWN + (number + 1) * FF, :].astype(BF16), arriving_low)
-        scaled = argument * math.sqrt(0.5)
-        twice_cdf = 1.0 + lax.erf(scaled)
-        bell = jnp.exp2(scaled * scaled * -math.log2(math.e)) * (2.0 / math.sqrt(math.pi))
+        back = back_v[part, :]
+        twice_cdf = 1.0 + lax.erf(argument * math.sqrt(0.5))
+        bell = jnp.exp2(argument * argument * (-0.5 * math.log2(math.e)) + 0.5 * math.log2(2.0 / math.pi))
         active = argument * twice_cdf
-        gate_grads.append(0.5 * jnp.sum(active * back, axis=0, keepdims=True))
-        hidden_v[part, :] = (active * gate).astype(BF16)
-        pre_v[part, :] = (back * gate * (twice_cdf + scaled * bell)).astype(BF16)
+        gated_grads.append(jnp.sum(active * back, axis=0, keepdims=True))
+        hidden_v[part, :] = active.astype(BF16)
+        pre_v[part, :] = (back * (twice_cdf + argument * bell)).astype(BF16)
         up = jnp.concatenate([shared_rows(ROW_UP + number * FF + half, 2) for half in range(2)], axis=1)
         more = dot(up, pre_v[part, :])
         upstream = more if upstream is None else upstream + more
-        if number + 1 < EXPERTS:
-            expert_sums(number)
-            if number:
-                advance(number - 1)
-
-    gate_grads = jnp.concatenate(gate_grads, axis=0)
-    g_logits = gates * (gate_grads - jnp.sum(gates * gate_grads, axis=0, keepdims=True))
+        if 0 < number < 3:
+            expert_sums(number - 1)
+        if number == 2:
+            advance(0)
+        if number == 3:
+            advance(1)
+
+    gated_grads = jnp.concatenate(gated_grads, axis=0)
+    g_logits = gated_grads - gates * jnp.sum(gated_grads, axis=0, keepdims=True)
     g_logits = jnp.concatenate([g_logits, jnp.zeros_like(g_logits)], axis=0).astype(BF16)
     g_after_self = arriving + norm_back(normed_three, inverse_three, gain_three, upstream)
     g_proj = g_after_self.astype(BF16)
@@ -582,45 +599,53 @@
     own_grad = folded(dot_points(self_weights, g_self_out))
     sent[2, 0:HEAD_DIM, :] = own_grad
     exchange(2).start()
-    expert_sums(EXPERTS - 1)
-    advance(2, 0)
+    expert_sums(2)
+    advance(0)
+    expert_sums(3)
+    g_queries = feature_softmax_back(self_soft, dot(self_low, g_self_out)).astype(BF16)
+    early.source[0:D, :] = dot_points(self_out, g_proj).astype(BF16)
+    early.source[D:, :] = dot_points(hidden_two, g_queries).astype(BF16)
+    early.begin()
+    advance(1, 2)
     router_sum = dot(g_logits, geometry_v[...])
     small = [None] * 6
     small[4] = to_row(over_points(upstream * normed_three))
     small[5] = to_row(over_points(upstream))
-    last.source[D : 2 * D, :] = dot_points(self_out, g_proj).astype(BF16)
-    g_queries = feature_softmax_back(self_soft, dot(self_low, g_self_out)).astype(BF16)
-    advance(3, 1)
+    query_part = dot(qkv_w[:, :D], g_queries)
+    advance(3, 4)
 
     exchange(2).wait_recv()
     scaled_grad = unfolded(own_grad + got[2, 0:HEAD_DIM, :]) * own_factor
     correction = over_points(scaled_grad * self_summary)
     g_keys = key_powers * (dot(scaled_grad.astype(BF16), self_values) - correction)
     g_values = dot(scaled_grad.T.astype(BF16), key_low)
-    g_qkv = jnp.concatenate([g_queries, g_keys.astype(BF16), g_values.astype(BF16)], axis=0)
-    upstream = dot(qkv_w, g_qkv)
+    g_keyval = jnp.concatenate([g_keys.astype(BF16), g_values.astype(BF16)], axis=0)
+    upstream = query_part + dot(qkv_w[:, D:], g_keyval)
+    keyval_sum = dot_points(hidden_two, g_keyval)
+    for half in range(2):
+        middle.source[half * D : (half + 1) * D, :] = keyval_sum[:, half * D : (half + 1) * D].astype(BF16)
+    middle.begin()
     g_after_cross = g_after_self + norm_back(normed_two, inverse_two, gain_two, upstream)
     g_proj = g_after_cross.astype(BF16)
     g_cross_out = dot(cross_w, g_proj).astype(BF16)
     own_mixed = folded(dot_points(cross_low, g_cross_out))
     sent[3, 0:HEAD_DIM, :] = own_mixed
     exchange(3).start()
-    advance(0, 2)
-    qkv_sum = dot_points(hidden_two, g_qkv)
-    for third in range(3):
-        middle.source[third * D : (third + 1) * D, :] = qkv_sum[:, third * D : (third + 1) * D].astype(BF16)
-    middle.source[3 * D :, :] = dot_points(cross_out, g_proj).astype(BF16)
-    middle.begin()
+    advance(0, 1)
+    last.source[D : 2 * D, :] = dot_points(cross_out, g_proj).astype(BF16)
     small[2] = to_row(over_points(upstream * normed_two))
     small[3] = to_row(over_points(upstream))
-
     g_query = feature_softmax_back(cross_soft, dot(mixed_low, g_cross_out)).astype(BF16)
-    advance(1, 3)
+    advance(5, 2)
     upstream_one = dot(query_w, g_query)
     last.source[0:D, :] = dot_points(hidden_one, g_query).astype(BF16)
     small[0] = to_row(over_points(upstream_one * normed_one))
     small[1] = to_row(over_points(upstream_one))
-    advance(4)
+    last.source[2 * D :, :] = jnp.concatenate(
+        [router_sum, *small, jnp.zeros((32 - 8 - len(small), D), F32)], axis=0
+    ).astype(BF16)
+    last.begin()
+    advance(3, 4)
 
     exchange(3).wait_recv()
     fn_grad = unfolded((own_mixed + got[3, 0:HEAD_DIM, :]) * fn_share)
@@ -629,32 +654,33 @@
     g_keys = fn_powers[...] * (dot(fn_scaled.astype(BF16), fn_values[...]) - fn_correction)
     g_values = dot(fn_scaled.T.astype(BF16), fn_low[...])
     g_keyval = jnp.concatenate([g_keys, g_values], axis=0).astype(BF16)
-    kv_sum = dot_points(fn_hidden[...], g_keyval)
+    normed_sum = dot_points(fn_normed[...], g_keyval)
+    plain_sum = dot_points(jnp.ones((8, fn_rows), BF16), g_keyval)[0:1]
+    kv_sum = branch_gain * normed_sum + branch_bias * plain_sum
     for half in range(2):
         branch.source[half * D : (half + 1) * D, :] = kv_sum[:, half * D : (half + 1) * D].astype(BF16)
+    kv_wide = kv.astype(F32)
+    branch.source[2 * D :, :] = jnp.concatenate(
+        [to_row(over_points(kv_wide * normed_sum)), to_row(over_points(kv_wide * plain_sum)), jnp.zeros((30, D), F32)],
+        axis=0,
+    ).astype(BF16)
     branch.begin()
-    upstream = dot(kv, g_keyval)
-    normed, _ = layer_norm(functions_v[...].astype(F32).T)
-    own_norm = [to_row(over_points(upstream * normed)), to_row(over_points(upstream))]
-    branch_norms = [jnp.where(fn == number, row, 0.0) for number in range(fns) for row in own_norm]
-    filled = 8 + len(small) + len(branch_norms)
-    last.source[2 * D :, :] = jnp.concatenate(
-        [router_sum, *small, *branch_norms, jnp.zeros((32 - filled, D), F32)], axis=0
-    ).astype(BF16)
-    last.begin()
-
     total = g_after_cross + norm_back(normed_one, inverse_one, gain_one, upstream_one)
     input_grad[...] = total.T.astype(BF16)
-    advance(0, 2, 1, 3)
+    advance(0, 1)
+    result = after_self
+    for number in range(EXPERTS):
+        part = slice(number * FF, (number + 1) * FF)
+        result = result + half_gates[number : number + 1] * dot(down_t[:, part], hidden_v[part, :])
+    output[...] = result.T.astype(BF16)
+    advance(5, 0, 2, 3, 4, 1)
+    last.advance()
     branch.advance()
-    last.advance()
-    result = after_self + dot(down_t[...], hidden_v[...])
-    output[...] = result.T.astype(BF16)
-    advance(4, 0, 1, 2, 3, 4, 0, 1, 2, 3, 4, 0, 1)
+    advance(0, 1, 2, 3, 4)
 
     for load in loads[6:]:
         load.wait()
-    waiting = [*experts, middle, branch, last]
+    waiting = [*experts, early, middle, last, branch]
 
     def finish(reduction):
         while reduction.steps_left:
@@ -678,22 +704,14 @@
         shared_sum[start : start + FF, :] = sums.total[FF:, :].astype(F32)
     whole = -(-ROW_UP // 16) * 16
     renew(whole, SHARED_ROWS - whole)
+    finish(early)
     finish(middle)
-    for third in range(3):
-        shared_sum[pl.ds(ROW_QKV + third, D, stride=3), :] = middle.total[
-            third * D : (third + 1) * D, :
-        ].astype(F32)
-    shared_sum[ROW_CROSS_OUT : ROW_CROSS_OUT + D, :] = middle.total[3 * D :, :].astype(F32)
-    finish(branch)
-    for half in range(2):
-        branch_rows[pl.ds(2 + half, D, stride=2), :] = branch.total[
-            half * D : (half + 1) * D, :
-        ].astype(F32)
-    for r in range(2, BRANCH_ROWS):
-        branch_sum[0:1, r * D : (r + 1) * D] = branch_rows[r : r + 1, :]
+    shared_sum[ROW_SELF_OUT : ROW_SELF_OUT + D, :] = early.total[0:D, :].astype(F32)
+    for third, held in enumerate([early.total[D:, :], middle.total[:D, :], middle.total[D:, :]]):
+        shared_sum[pl.ds(ROW_QKV + third, D, stride=3), :] = held.astype(F32)
     finish(last)
     shared_sum[ROW_QUERY : ROW_QUERY + D, :] = last.total[0:D, :].astype(F32)
-    shared_sum[ROW_SELF_OUT : ROW_SELF_OUT + D, :] = last.total[D : 2 * D, :].astype(F32)
+    shared_sum[ROW_CROSS_OUT : ROW_CROSS_OUT + D, :] = last.total[D : 2 * D, :].astype(F32)
     rest = last.total[2 * D :, :].astype(F32)
     for at, row in enumerate(
         [ROW_GAIN_ONE, ROW_BIAS_ONE, ROW_GAIN_TWO, ROW_BIAS_TWO, ROW_GAIN_THREE, ROW_BIAS_THREE]
@@ -707,11 +725,14 @@
             jnp.where(router_mask, spread, 0.0), axis=0, keepdims=True
         )
     renew(0, whole)
-    own_norm = rest[14:16]
-    for number in range(1, fns):
-        own_norm = jnp.where(fn == number, rest[14 + 2 * number : 16 + 2 * number], own_norm)
-    for r in range(2):
-        branch_sum[0:1, r * D : (r + 1) * D] = own_norm[r : r + 1]
+    finish(branch)
+    for half in range(2):
+        branch_rows[pl.ds(2 + half, D, stride=2), :] = branch.total[
+            half * D : (half + 1) * D, :
+        ].astype(F32)
+    branch_rows[0:2, :] = branch.total[2 * D :, :].astype(F32)[0:2]
+    for r in range(BRANCH_ROWS):
+        branch_sum[0:1, r * D : (r + 1) * D] = branch_rows[r : r + 1, :]
     new = sgd_update(*(ref[...] for ref in branch_new[:3]), branch_sum[...], branch_rate)
     for value, target in zip(new, branch_new):
         target[...] = value
@@ -750,7 +771,7 @@
     scratch = [low(rows, D), low(rows, D), low(fn_rows, D), low(rows, D)]
     scratch += [wide(BRANCH_ROWS, D), wide(SHARED_ROWS, D), wide(*branch)]
     scratch += [wide(D, fn_rows), low(D, fn_rows), low(D, fn_rows), low(D, fn_rows), low(HIDDEN, rows), low(HIDDEN, rows)]
-    scratch += [wide(max(EARLY_BACK, 1) * FF, rows), low(HIDDEN, D), low(D, HIDDEN)]
+    scratch += [wide(HIDDEN, rows), low(EXPERTS * D, rows), low(HIDDEN, D), low(D, HIDDEN)]
     scratch += [wide(4, HEAD_DIM + 8, D), wide(4, HEAD_DIM + 8, D)]
     scratch += [pltpu.SemaphoreType.DMA((10,)), pltpu.SemaphoreType.DMA((4,)), pltpu.SemaphoreType.DMA((4,))]
     for reduction in plan(fns, pts):

time: 57.9 us -> 53.7 us (0.927)
  Pallas kernels: 55 us -> 50.8 us
    pallas_call x1, Pallas kernels: 52.1 us -> 47.9 us  [whole_step(): pl.pallas_call(functools.partial(step_kernel, fns, pts, *rates), out_shap...]
where the time goes in v4:
time: 53.7 us; the launch traced here: 53.5 us
  Pallas kernels  50.8 us (95%)
  between operations  2.75 us (5%)
    pallas_call x1, Pallas kernels, whole_step(): pl.pallas_call(functools.partial(step_kernel, fns, pts, *rates), out_shap...  47.9 us
    pallas_call x1, Pallas kernels, stored(): pl.pallas_call(functools.partial(store_kernel, count), out_shape=[jax.Sha...  2.88 us

profile of v4, /device:TPU:0, one launch (start us, length us, event | category | flops | bytes accessed | tf_op | source)
XLA Modules:
  0.0 53.5 jit_solution(7812819970002263467)
XLA Ops:
  2.6 47.9 %shard_map.212 = (bf16[2048,128]{1,0:T(8,128)(2,1)S(1)}, bf16[2048,128]{1,0:T(8,128)(2,1)S(1)}, f32[2826,128]{1,0:T(8,128)S(1)}, f32[2826,128]{1,0:T(8,128)S(1)}...) custom-call(s32[1,1]{1,0:T(1,128)S(6)} %copy.24.refs_0_, ...), custom_call_target="tpu_custom_call" | custom-call | tf_op jit(solution)/shard_map/pallas_call | solution.py:779
  50.5 2.9 %shard_map.213 = (bf16[2048,128]{1,0:T(8,128)(2,1)}, bf16[2048,128]{1,0:T(8,128)(2,1)}, f32[2826,128]{1,0:T(8,128)}, f32[2826,128]{1,0:T(8,128)}, f32[2826,128]{...) custom-call(bf16[2048,128]{1,0:T(8,128)(2,1)S(1)} %get-tuple-element, ...), custom_call_target="tpu_custom_call" | custom-call | tf_op jit(solution)/shard_map/pallas_call | solution.py:804

commit v5 on v4

--- a/solution.py
+++ b/solution.py
@@ -40,9 +40,8 @@
 BRANCH_ROWS = 2 + 2 * D
 
 EXPERT_ROWS = 2 * FF
-EARLY_ROWS = 2 * D
-MIDDLE_ROWS = 2 * D
-LAST_ROWS = 2 * D + 32
+MIDDLE_ROWS = 4 * D
+LAST_ROWS = 2 * D + 16
 BRANCH_SENT = 2 * D + 32
 
 VMEM_LIMIT = 52
@@ -57,14 +56,33 @@
 
 
 class Level:
-    def __init__(self, size, index, member):
-        self.size, self.index, self.member = size, index, member
+    def __init__(self, grid, member):
+        sizes = [size for size, _ in grid]
+        self.size = math.prod(sizes)
+        shifted = [
+            [at if by == 0 else lax.rem(at + by, size) for by in range(size)] if size > 1 else [0]
+            for size, at in grid
+        ]
+        self.peers = []
+        for k in range(self.size):
+            place, index, left = [], 0, k
+            for size, moved in zip(reversed(sizes), reversed(shifted)):
+                place.append(moved[left % size])
+                left //= size
+            place.reverse()
+            for size, at in zip(sizes, place):
+                index = index * size + at
+            self.peers.append((index, member(*place)))
+        self.index = self.peers[0][0]
+
+
+TILE = 16
 
 
 def split_rows(rows, size):
-    step = 16
+    step = TILE
     while rows % step or rows // step > size:
-        step += 16
+        step += TILE
     return step, rows // step
 
 
@@ -148,7 +166,7 @@
             dst_ref=window.at[pl.ds(0, rows), :],
             send_sem=self.parts[at][2].at[sem],
             recv_sem=self.parts[at][2].at[sem],
-            device_id=self.levels[at].member(self.levels[at].index),
+            device_id=self.levels[at].peers[0][1],
             device_id_type=MESH,
         )
         (copy.wait_send if sending else copy.wait_recv)()
@@ -158,23 +176,20 @@
         received, _, sems = self.parts[at]
 
         def go():
-            def one(k, carry):
-                peer = (level.index + k) % level.size
+            for k in range(1, level.size):
+                peer, device = level.peers[k]
 
                 def start():
                     pltpu.make_async_remote_copy(
-                        src_ref=self.rows_from(at).at[pl.ds(pl.multiple_of(peer * step, 16), step), :],
-                        dst_ref=received.at[pl.ds(pl.multiple_of((k - 1) * step, 16), step), :],
+                        src_ref=self.rows_from(at).at[pl.ds(pl.multiple_of(peer * step, TILE), step), :],
+                        dst_ref=received.at[pl.ds((k - 1) * step, step), :],
                         send_sem=sems.at[0],
                         recv_sem=sems.at[1],
-                        device_id=level.member(peer),
+                        device_id=device,
                         device_id_type=MESH,
                     ).start()
 
                 self.when(None if owners == level.size else peer < owners, start)
-                return carry
-
-            lax.fori_loop(1, level.size, one, 0)
 
         self.when(self.inside(at), go)
 
@@ -184,14 +199,14 @@
         def go():
             received, kept, _ = self.parts[at]
             self.wait(at, 1, (level.size - 1) * step, False)
-            start = pl.multiple_of(level.index * step, 16)
+            start = pl.multiple_of(level.index * step, TILE)
             total = self.rows_from(at)[pl.ds(start, step), :].astype(F32)
             for k in range(level.size - 1):
                 total = total + received[k * step : (k + 1) * step, :].astype(F32)
             if at + 1 < len(self.sizes):
                 kept[...] = total.astype(BF16)
             else:
-                self.total[pl.ds(pl.multiple_of(self.base(at) + start, 16), step), :] = total.astype(BF16)
+                self.total[pl.ds(pl.multiple_of(self.base(at) + start, TILE), step), :] = total.astype(BF16)
 
         self.split(at, go, None)
 
@@ -200,20 +215,17 @@
         sems = self.parts[at][2]
 
         def go():
-            rows = pl.ds(pl.multiple_of(self.base(at) + level.index * step, 16), step)
-
-            def one(k, carry):
+            rows = pl.ds(pl.multiple_of(self.base(at) + level.index * step, TILE), step)
+
+            for _, device in level.peers[1:]:
                 pltpu.make_async_remote_copy(
                     src_ref=self.total.at[rows, :],
                     dst_ref=self.total.at[rows, :],
                     send_sem=sems.at[2],
                     recv_sem=sems.at[3],
-                    device_id=level.member((level.index + k) % level.size),
+                    device_id=device,
                     device_id_type=MESH,
                 ).start()
-                return carry
-
-            lax.fori_loop(1, level.size, one, 0)
 
         self.split(at, go, None)
 
@@ -259,7 +271,6 @@
         Reduction(stepwise, EXPERT_ROWS),
         Reduction(halved, EXPERT_ROWS),
         Reduction(halved, EXPERT_ROWS),
-        Reduction(halved, EARLY_ROWS),
         Reduction(halved, MIDDLE_ROWS),
         Reduction(at_once, LAST_ROWS),
         Reduction(items, BRANCH_SENT),
@@ -323,49 +334,35 @@
     assert not refs
 
     fn, pt = lax.axis_index("fn"), lax.axis_index("pts")
-    core_size, middle_size_ = inner_size(pts), middle_size(pts)
-    near_size = core_size * middle_size_
-    far, near = pt // near_size, pt % near_size
-    middle_at, core = near // core_size, near % core_size
-    far_level = Level(pts // near_size, far, lambda j: (fn, j * near_size + near))
+    core_size, mid_size = inner_size(pts), middle_size(pts)
+    near_size = core_size * mid_size
+    far, near = lax.div(pt, near_size), lax.rem(pt, near_size)
+    mid, core = lax.div(near, core_size), lax.rem(near, core_size)
+
+    def item(far_at, mid_at, core_at):
+        return far_at * near_size + mid_at * core_size + core_at
+
+    fn_axis, far_axis, mid_axis, core_axis = (fns, fn), (pts // near_size, far), (mid_size, mid), (core_size, core)
+    far_level = Level([far_axis], lambda z: (fn, item(z, mid, core)))
     stepwise = [
-        Level(core_size, core, lambda j: (fn, pt - core + j)),
-        Level(
-            fns * middle_size_,
-            fn * middle_size_ + middle_at,
-            lambda j: (j // middle_size_, far * near_size + j % middle_size_ * core_size + core),
-        ),
+        Level([core_axis], lambda c: (fn, item(far, mid, c))),
+        Level([fn_axis, mid_axis], lambda f, m: (f, item(far, m, core))),
         far_level,
     ]
     if fns * pts <= 32:
-        outer = pts // core_size
-        halved = [
-            stepwise[0],
-            Level(
-                fns * outer,
-                fn * outer + pt // core_size,
-                lambda j: (j // outer, j % outer * core_size + core),
-            ),
-        ]
-        at_once = [Level(fns * pts, fn * pts + pt, lambda j: (j // pts, j % pts))]
-        items = [Level(pts, pt, lambda j: (fn, j))]
+        halved = [stepwise[0], Level([fn_axis, far_axis, mid_axis], lambda f, z, m: (f, item(z, m, core)))]
+        at_once = [Level([fn_axis, far_axis, mid_axis, core_axis], lambda f, z, m, c: (f, item(z, m, c)))]
+        items = [Level([far_axis, mid_axis, core_axis], lambda z, m, c: (fn, item(z, m, c)))]
         greeted = at_once
     else:
         halved = at_once = stepwise
-        items = [Level(near_size, near, lambda j: (fn, far * near_size + j)), far_level]
-        greeted = [
-            Level(
-                fns * near_size,
-                fn * near_size + near,
-                lambda j: (j // near_size, far * near_size + j % near_size),
-            ),
-            far_level,
-        ]
-    ways = [stepwise, stepwise, halved, halved, halved, halved, at_once, items]
+        items = [Level([mid_axis, core_axis], lambda m, c: (fn, item(far, m, c))), far_level]
+        greeted = [Level([fn_axis, mid_axis, core_axis], lambda f, m, c: (f, item(far, m, c))), far_level]
+    ways = [stepwise, stepwise, halved, halved, halved, at_once, items]
     for reduction, scratch, levels in zip(reductions, bound, ways):
         reduction.bind(scratch, levels)
     experts = reductions[:EXPERTS]
-    early, middle, last, branch = reductions[EXPERTS:]
+    middle, last, branch = reductions[EXPERTS:]
 
     rows, fn_rows = points_v.shape[0], functions_v.shape[0]
 
@@ -386,17 +383,8 @@
 
     barrier = pltpu.get_barrier_semaphore()
     for level in greeted:
-
-        def greet(k, carry, level=level):
-            pl.semaphore_signal(
-                barrier,
-                inc=1,
-                device_id=level.member((level.index + k) % level.size),
-                device_id_type=MESH,
-            )
-            return carry
-
-        lax.fori_loop(1, level.size, greet, 0)
+        for _, device in level.peers[1:]:
+            pl.semaphore_signal(barrier, inc=1, device_id=device, device_id_type=MESH)
 
     def exchange(at):
         return pltpu.make_async_remote_copy(
@@ -404,7 +392,7 @@
             dst_ref=got.at[at],
             send_sem=x_send.at[at],
             recv_sem=x_recv.at[at],
-            device_id=((fn + 1) % fns, pt),
+            device_id=(lax.rem(fn + 1, fns), pt),
             device_id_type=MESH,
         )
 
@@ -603,16 +591,15 @@
     advance(0)
     expert_sums(3)
     g_queries = feature_softmax_back(self_soft, dot(self_low, g_self_out)).astype(BF16)
-    early.source[0:D, :] = dot_points(self_out, g_proj).astype(BF16)
-    early.source[D:, :] = dot_points(hidden_two, g_queries).astype(BF16)
-    early.begin()
+    middle.source[2 * D : 3 * D, :] = dot_points(self_out, g_proj).astype(BF16)
+    middle.source[3 * D :, :] = dot_points(hidden_two, g_queries).astype(BF16)
     advance(1, 2)
     router_sum = dot(g_logits, geometry_v[...])
     small = [None] * 6
     small[4] = to_row(over_points(upstream * normed_three))
     small[5] = to_row(over_points(upstream))
     query_part = dot(qkv_w[:, :D], g_queries)
-    advance(3, 4)
+    advance(3)
 
     exchange(2).wait_recv()
     scaled_grad = unfolded(own_grad + got[2, 0:HEAD_DIM, :]) * own_factor
@@ -631,21 +618,21 @@
     own_mixed = folded(dot_points(cross_low, g_cross_out))
     sent[3, 0:HEAD_DIM, :] = own_mixed
     exchange(3).start()
-    advance(0, 1)
+    advance(0)
     last.source[D : 2 * D, :] = dot_points(cross_out, g_proj).astype(BF16)
     small[2] = to_row(over_points(upstream * normed_two))
     small[3] = to_row(over_points(upstream))
     g_query = feature_softmax_back(cross_soft, dot(mixed_low, g_cross_out)).astype(BF16)
-    advance(5, 2)
+    advance(4)
     upstream_one = dot(query_w, g_query)
     last.source[0:D, :] = dot_points(hidden_one, g_query).astype(BF16)
     small[0] = to_row(over_points(upstream_one * normed_one))
     small[1] = to_row(over_points(upstream_one))
     last.source[2 * D :, :] = jnp.concatenate(
-        [router_sum, *small, jnp.zeros((32 - 8 - len(small), D), F32)], axis=0
+        [router_sum, *small, jnp.zeros((2, D), F32)], axis=0
     ).astype(BF16)
     last.begin()
-    advance(3, 4)
+    advance(1)
 
     exchange(3).wait_recv()
     fn_grad = unfolded((own_mixed + got[3, 0:HEAD_DIM, :]) * fn_share)
@@ -667,20 +654,19 @@
     branch.begin()
     total = g_after_cross + norm_back(normed_one, inverse_one, gain_one, upstream_one)
     input_grad[...] = total.T.astype(BF16)
-    advance(0, 1)
     result = after_self
     for number in range(EXPERTS):
         part = slice(number * FF, (number + 1) * FF)
         result = result + half_gates[number : number + 1] * dot(down_t[:, part], hidden_v[part, :])
     output[...] = result.T.astype(BF16)
-    advance(5, 0, 2, 3, 4, 1)
+    advance(2, 3, 0, 1, 4)
     last.advance()
     branch.advance()
-    advance(0, 1, 2, 3, 4)
+    advance(0, 1, 2, 3)
 
     for load in loads[6:]:
         load.wait()
-    waiting = [*experts, early, middle, last, branch]
+    waiting = [*experts, middle, last, branch]
 
     def finish(reduction):
         while reduction.steps_left:
@@ -704,10 +690,9 @@
         shared_sum[start : start + FF, :] = sums.total[FF:, :].astype(F32)
     whole = -(-ROW_UP // 16) * 16
     renew(whole, SHARED_ROWS - whole)
-    finish(early)
     finish(middle)
-    shared_sum[ROW_SELF_OUT : ROW_SELF_OUT + D, :] = early.total[0:D, :].astype(F32)
-    for third, held in enumerate([early.total[D:, :], middle.total[:D, :], middle.total[D:, :]]):
+    shared_sum[ROW_SELF_OUT : ROW_SELF_OUT + D, :] = middle.total[2 * D : 3 * D, :].astype(F32)
+    for third, held in enumerate([middle.total[3 * D :, :], middle.total[:D, :], middle.total[D : 2 * D, :]]):
         shared_sum[pl.ds(ROW_QKV + third, D, stride=3), :] = held.astype(F32)
     finish(last)
     shared_sum[ROW_QUERY : ROW_QUERY + D, :] = last.total[0:D, :].astype(F32)

time: 53.7 us -> 50.8 us (0.946)
  Pallas kernels: 50.8 us -> 47.9 us
    pallas_call x1, Pallas kernels: 47.9 us -> 45 us  [whole_step(): pl.pallas_call(functools.partial(step_kernel, fns, pts, *rates), out_shap...]
where the time goes in v5:
time: 50.8 us; the launch traced here: 50.7 us
  Pallas kernels  47.9 us (94%)
  between operations  2.75 us (5%)
    pallas_call x1, Pallas kernels, whole_step(): pl.pallas_call(functools.partial(step_kernel, fns, pts, *rates), out_shap...  45 us
    pallas_call x1, Pallas kernels, stored(): pl.pallas_call(functools.partial(store_kernel, count), out_shape=[jax.Sha...  2.88 us

profile of v5, /device:TPU:0, one launch (start us, length us, event | category | flops | bytes accessed | tf_op | source)
XLA Modules:
  0.0 50.7 jit_solution(895751811396864190)
XLA Ops:
  2.6 45.0 %shard_map.212 = (bf16[2048,128]{1,0:T(8,128)(2,1)S(1)}, bf16[2048,128]{1,0:T(8,128)(2,1)S(1)}, f32[2826,128]{1,0:T(8,128)S(1)}, f32[2826,128]{1,0:T(8,128)S(1)}...) custom-call(s32[1,1]{1,0:T(1,128)S(6)} %copy.24.refs_0_, ...), custom_call_target="tpu_custom_call" | custom-call | tf_op jit(solution)/shard_map/pallas_call | solution.py:764
  47.6 2.9 %shard_map.213 = (bf16[2048,128]{1,0:T(8,128)(2,1)}, bf16[2048,128]{1,0:T(8,128)(2,1)}, f32[2826,128]{1,0:T(8,128)}, f32[2826,128]{1,0:T(8,128)}, f32[2826,128]{...) custom-call(bf16[2048,128]{1,0:T(8,128)(2,1)S(1)} %get-tuple-element, ...), custom_call_target="tpu_custom_call" | custom-call | tf_op jit(solution)/shard_map/pallas_call | solution.py:789

commit v6 on v5

--- a/solution.py
+++ b/solution.py
@@ -499,10 +499,10 @@
     after_cross = points + dot(cross_w.T, cross_out)
     normed_two, inverse_two = layer_norm(after_cross)
     hidden_two = (normed_two * gain_two + bias_two).astype(BF16)
-    qkv = dot(qkv_w.T, hidden_two)
+    qkv = dot(qkv_w[:, D:].T, hidden_two)
     usable = lax.broadcasted_iota(jnp.int32, (1, rows), 1) + fn * rows < item_counts[0]
-    keys = jnp.where(usable, qkv[D : 2 * D], far_below)
-    self_values = qkv[2 * D :].astype(BF16)
+    keys = jnp.where(usable, qkv[:D], far_below)
+    self_values = qkv[D:].astype(BF16)
     key_max = jnp.max(keys, axis=1, keepdims=True)
     key_powers = jnp.where(usable, jnp.exp(keys - key_max), 0.0)
     key_low = key_powers.astype(BF16)
@@ -514,7 +514,7 @@
     )
     exchange(1).start()
 
-    self_soft = feature_softmax(qkv[:D])
+    self_soft = feature_softmax(dot(qkv_w[:, :D].T, hidden_two))
     self_weights = self_soft.astype(BF16)
     loads[4].wait()
     logits = dot_points(router_t, geometry_v[...])[:EXPERTS]
@@ -594,10 +594,7 @@
     middle.source[2 * D : 3 * D, :] = dot_points(self_out, g_proj).astype(BF16)
     middle.source[3 * D :, :] = dot_points(hidden_two, g_queries).astype(BF16)
     advance(1, 2)
-    router_sum = dot(g_logits, geometry_v[...])
-    small = [None] * 6
-    small[4] = to_row(over_points(upstream * normed_three))
-    small[5] = to_row(over_points(upstream))
+    upstream_three = upstream
     query_part = dot(qkv_w[:, :D], g_queries)
     advance(3)
 
@@ -620,6 +617,10 @@
     exchange(3).start()
     advance(0)
     last.source[D : 2 * D, :] = dot_points(cross_out, g_proj).astype(BF16)
+    router_sum = dot(g_logits, geometry_v[...])
+    small = [None] * 6
+    small[4] = to_row(over_points(upstream_three * normed_three))
+    small[5] = to_row(over_points(upstream_three))
     small[2] = to_row(over_points(upstream * normed_two))
     small[3] = to_row(over_points(upstream))
     g_query = feature_softmax_back(cross_soft, dot(mixed_low, g_cross_out)).astype(BF16)
@@ -710,22 +711,23 @@
             jnp.where(router_mask, spread, 0.0), axis=0, keepdims=True
         )
     renew(0, whole)
+    for at in range(4):
+        exchange(at).wait_send()
+    for reduction in [*experts, middle]:
+        reduction.drain()
     finish(branch)
-    for half in range(2):
-        branch_rows[pl.ds(2 + half, D, stride=2), :] = branch.total[
-            half * D : (half + 1) * D, :
-        ].astype(F32)
-    branch_rows[0:2, :] = branch.total[2 * D :, :].astype(F32)[0:2]
-    for r in range(BRANCH_ROWS):
-        branch_sum[0:1, r * D : (r + 1) * D] = branch_rows[r : r + 1, :]
+    branch_rows[0 : 2 * D, :] = branch.total[0 : 2 * D, :].astype(F32)
+    branch_rows[2 * D :, :] = branch.total[2 * D :, :].astype(F32)[0:2]
+    for r in range(2):
+        branch_sum[0:1, r * D : (r + 1) * D] = branch_rows[2 * D + r : 2 * D + r + 1, :]
+    for r in range(2 * D):
+        branch_sum[0:1, (r + 2) * D : (r + 3) * D] = branch_rows[r % 2 * D + r // 2 : r % 2 * D + r // 2 + 1, :]
     new = sgd_update(*(ref[...] for ref in branch_new[:3]), branch_sum[...], branch_rate)
     for value, target in zip(new, branch_new):
         target[...] = value
 
-    for at in range(4):
-        exchange(at).wait_send()
-    for reduction in reductions:
-        reduction.drain()
+    last.drain()
+    branch.drain()
 
 
 def sgd_update(weights, momentum, average, gradient, step_rate):

time: 50.8 us -> 50.6 us (level)
  no operation moved by 1% of the time
where the time goes in v6:
time: 50.6 us; the launch traced here: 50.5 us
  Pallas kernels  47.7 us (94%)
  between operations  2.75 us (5%)
    pallas_call x1, Pallas kernels, whole_step(): pl.pallas_call(functools.partial(step_kernel, fns, pts, *rates), out_shap...  44.8 us
    pallas_call x1, Pallas kernels, stored(): pl.pallas_call(functools.partial(store_kernel, count), out_shape=[jax.Sha...  2.88 us

profile of v6, /device:TPU:0, one launch (start us, length us, event | category | flops | bytes accessed | tf_op | source)
XLA Modules:
  0.0 50.5 jit_solution(11463256001139267447)
XLA Ops:
  2.6 44.8 %shard_map.212 = (bf16[2048,128]{1,0:T(8,128)(2,1)S(1)}, bf16[2048,128]{1,0:T(8,128)(2,1)S(1)}, f32[2826,128]{1,0:T(8,128)S(1)}, f32[2826,128]{1,0:T(8,128)S(1)}...) custom-call(s32[1,1]{1,0:T(1,128)S(6)} %copy.24.refs_0_, ...), custom_call_target="tpu_custom_call" | custom-call | tf_op jit(solution)/shard_map/pallas_call | solution.py:766
  47.4 2.9 %shard_map.213 = (bf16[2048,128]{1,0:T(8,128)(2,1)}, bf16[2048,128]{1,0:T(8,128)(2,1)}, f32[2826,128]{1,0:T(8,128)}, f32[2826,128]{1,0:T(8,128)}, f32[2826,128]{...) custom-call(bf16[2048,128]{1,0:T(8,128)(2,1)S(1)} %get-tuple-element, ...), custom_call_target="tpu_custom_call" | custom-call | tf_op jit(solution)/shard_map/pallas_call | solution.py:791
